TPU v7x, 256 devices: a whole 4x4x8 slice. The times are simulated.
256 devices in a mesh: grp: 32 (over y, x, core), mem: 8 (over z).
Axes of the slice: x: 4, y: 4, z: 8, core: 2. Of those that a mesh axis runs over, the one named last changes fastest.
Arguments:
- voxels: bfloat16 [32768, 6, 6, 384], P(('grp', 'mem')), may hold values from -6 to 6
- conv_weight: bfloat16 [3, 3, 3, 64, 64], replicated, may hold values from -0.15625 to 0.15625
- conv_bias: float32 [64], replicated, may hold values from -3 to 3
- row_counts: int32 [256], P(('grp', 'mem')), may hold values from 512 to 2048, as said below
- sample_patch: int32 [524288], P(('grp', 'mem')), may hold values from 0 to 31
- targets: float32 [524288], P(('grp', 'mem')), may hold values from -6 to 6
- query_patch: int32 [16384], P(('grp', 'mem')), may hold values from 0 to 127
Outputs:
- post_var: float32 [32, 8, 2048], P('grp', 'mem')
- post_mean: float32 [32, 8, 2048], P('grp', 'mem')
Inputs may be any that keep to these rules, and one draw needn't show every extreme that they name: row_counts[d] is the number of live leading rows of device d; some device has all 2048 rows live.
All inputs are finite; a program needn't handle non-finite values.
Results may differ from a plain program's by a relative error of at most 0.0052.
Values may be sent and summed in bfloat16 or wider, within the bound.
A program may use at most 64 MiB of HBM per device.

v0:
```python
import jax
import jax.numpy as jnp
from jax import lax
from jax.sharding import PartitionSpec as P

C = 64
EDGE = 6


noise_scale = 8.0


def tri_solve(lower, rhs, transposed):
    return lax.linalg.triangular_solve(
        lower, rhs, left_side=True, lower=True, transpose_a=transposed
    )


def features_of(volume, conv_weight, conv_bias):
    patch_count = volume.shape[0]
    shaped = volume.reshape(patch_count, EDGE, EDGE, EDGE, C)
    convolved = lax.conv_general_dilated(
        shaped,
        conv_weight,
        (1, 1, 1),
        "VALID",
        dimension_numbers=("NDHWC", "DHWIO", "NDHWC"),
        preferred_element_type=jnp.float32,
    )
    activated = jnp.tanh(convolved + conv_bias).reshape(patch_count, 2, 2, 2, 2, 2, 2, C)
    pooled = jnp.mean(activated, axis=(2, 4, 6))
    return pooled.reshape(patch_count, 8 * C)


def hit_sums(patch_ids, target_part, live_count, patch_count):
    row_total = patch_ids.shape[0]
    live_mask = (jnp.arange(row_total, dtype=jnp.int32) < live_count).astype(jnp.float32)
    onehot = (jnp.arange(patch_count, dtype=jnp.int32)[:, None] == patch_ids[None, :]).astype(
        jnp.float32
    )
    paired = jnp.stack([live_mask, live_mask * target_part])
    summed = jnp.einsum("pr,kr->kp", onehot, paired, precision=lax.Precision.HIGHEST)
    return (summed[0], summed[1])


def weighted_gram(patch_feats, hits, target_sum):
    gram_part = jnp.dot(
        (patch_feats * hits[:, None]).T,
        patch_feats,
        precision=lax.Precision.HIGHEST,
        preferred_element_type=jnp.float32,
    )
    moment = jnp.dot(
        target_sum, patch_feats, precision=lax.Precision.HIGHEST, preferred_element_type=jnp.float32
    )
    return (gram_part, moment)


def on_device(voxels, conv_weight, conv_bias, row_counts, sample_patch, targets, query_patch):
    patch_feats = features_of(voxels, conv_weight, conv_bias)
    feat_width = patch_feats.shape[1]
    queries = jnp.take(patch_feats, query_patch, axis=0).astype(jnp.bfloat16)
    gathered = lax.all_gather(queries, "grp", axis=0, tiled=True)
    hits, target_sum = hit_sums(sample_patch, targets, row_counts[0], patch_feats.shape[0])
    gram_part, moment = weighted_gram(patch_feats, hits, target_sum)
    gram_whole, moment_whole = lax.psum((gram_part, moment), "mem")
    precision_matrix = jnp.eye(feat_width, dtype=jnp.float32) + gram_whole / noise_scale
    lower = jnp.linalg.cholesky(precision_matrix)
    half_solve = tri_solve(lower, (moment_whole / noise_scale)[:, None], False)
    weights = tri_solve(lower, half_solve, True)[:, 0]
    query_float = gathered.astype(jnp.float32)
    whitened = tri_solve(lower, query_float.T, False)
    variances = jnp.sum(whitened * whitened, axis=0)
    means = jnp.dot(
        query_float, weights, precision=lax.Precision.HIGHEST, preferred_element_type=jnp.float32
    )
    column_count = query_float.shape[0]
    return (variances.reshape(1, 1, column_count), means.reshape(1, 1, column_count))


def solution(mesh):
    in_specs = (
        P(("grp", "mem"), None, None, None),
        P(),
        P(),
        P(("grp", "mem")),
        P(("grp", "mem")),
        P(("grp", "mem")),
        P(("grp", "mem")),
    )
    out_specs = (P("grp", "mem", None), P("grp", "mem", None))
    return jax.shard_map(
        on_device, mesh=mesh, in_specs=in_specs, out_specs=out_specs, check_vma=False
    )
```

profile of v0, /device:TPU:2, one launch (start us, length us, event | category | flops | bytes accessed | tf_op | source)
XLA Modules:
  0.0 276.9 jit_solution(2330563505799783818)
XLA Ops:
  9.5 1.3 fusion.26
  10.8 6.0 %copy.12 = bf16[128,6,6,384]{0,3,2,1:T(8,128)(2,1)} copy(bf16[128,6,6,384]{3,0,2,1:T(8,128)(2,1)} %param.7) | data formatting | bytes 7077888 | tf_op args[0]
  16.8 7.1 %add_tanh_fusion = f32[128,4,4,4,64]{0,4,3,2,1:T(8,128)S(1)} fusion(bf16[128,6,6,6,64]{0,4,3,2,1:T(8,128)(2,1)} %bitcast.178, bf16[3,3,3,64,64]{4,3,2,1,0:T(8,128)(2,1)S(1)} %copy-done, f32[64]{0:T(128)S(1)} %copy-done.4), kind=kOutput, calls=%fused_computation.18 | convolution fusion | flops 1812463616 | bytes 5857536 | tf_op jit(solution)/shard_map/conv_general_dilated | solution.py:22
  24.2 2.0 fusion.98
  28.1 20.2 %psum.15 = f32[512]{0:T(512)S(1)} all-reduce(f32[512]{0:T(512)S(1)} %bitcast.186), channel_id=1, replica_groups=mesh['grp'=32,'mem'=8] {'mem'}, use_global_device_ids=true, to_apply=%region_11.12 | all-reduce | flops 512 | bytes 4096 | tf_op jit(solution)/shard_map/psum | solution.py:66
  48.3 56.9 %all-reduce.3.cloned.1.call-done = f32[512,512]{0,1:T(8,128)} async-done(((f32[512,512]{0,1:T(8,128)}), f32[512,512]{0,1:T(8,128)}) %all-reduce.3.cloned.1.call-update) | async-done | bytes 1048592 | tf_op jit(solution)/shard_map/psum | solution.py:66
  105.2 2.4 multiply_add_fusion
  107.6 1.6 copy.14
  110.5 11.7 %cholesky.104 = f32[128,128]{1,0:T(8,128)S(1)} custom-call(f32[128,128]{1,0:T(8,128)S(1)} %cholesky.266), custom_call_target="Cholesky" | custom-call | tf_op jit(solution)/shard_map/jit(cholesky)/cholesky | solution.py:68
  122.3 9.8 %custom-call.34 = f32[1,128,128]{1,2,0:T(8,128)S(1)} custom-call(f32[1,128,128]{2,1,0:T(8,128)S(1)} %get-tuple-element.31), custom_call_target="InvertDiagBlocksLowerTriangular" | custom-call | tf_op jit(solution)/shard_map/jit(cholesky)/cholesky | solution.py:68
  132.2 1.2 constant_dynamic-update-slice_fusion.3
  133.4 1.3 convolution_subtract_fusion.2
  134.7 11.7 %cholesky.217 = f32[128,128]{1,0:T(8,128)S(1)} custom-call(f32[128,128]{1,0:T(8,128)S(1)} %cholesky.270), custom_call_target="Cholesky" | custom-call | tf_op jit(solution)/shard_map/jit(cholesky)/cholesky | solution.py:68
  146.4 10.2 %custom-call.35 = f32[1,128,128]{1,2,0:T(8,128)S(1)} custom-call(f32[1,128,128]{2,1,0:T(8,128)S(1)} %get-tuple-element.28), custom_call_target="InvertDiagBlocksLowerTriangular" | custom-call | tf_op jit(solution)/shard_map/jit(cholesky)/cholesky | solution.py:68
  156.9 1.3 convolution_subtract_fusion.3
  158.2 11.7 %cholesky.238 = f32[128,128]{1,0:T(8,128)S(1)} custom-call(f32[128,128]{1,0:T(8,128)S(1)} %cholesky.275), custom_call_target="Cholesky" | custom-call | tf_op jit(solution)/shard_map/jit(cholesky)/cholesky | solution.py:68
  170.5 9.8 %custom-call.36 = f32[1,128,128]{1,2,0:T(8,128)S(1)} custom-call(f32[1,128,128]{2,1,0:T(8,128)S(1)} %get-tuple-element.25), custom_call_target="InvertDiagBlocksLowerTriangular" | custom-call | tf_op jit(solution)/shard_map/jit(cholesky)/cholesky | solution.py:68
  180.6 1.2 convolution_subtract_fusion.4
  181.8 11.7 %cholesky.255 = f32[128,128]{1,0:T(8,128)S(1)} custom-call(f32[128,128]{1,0:T(8,128)S(1)} %convolution_subtract_fusion.4), custom_call_target="Cholesky" | custom-call | tf_op jit(solution)/shard_map/jit(cholesky)/cholesky | solution.py:68
  197.7 7.9 %while.1 = (s32[]{:T(128)}, f32[512,512]{1,0:T(8,128)S(1)}, s32[4,2]{0,1:T(2,128)S(1)}, f32[4,128,128]{2,1,0:T(8,128)S(1)}, s32[]{:T(128)}) while((s32[]{:T(128)}, f32[512,512]{1,0:T(8,128)S(1)}, s32[4,2]{0,1:T(2,128)S(1)}, f32[4,128,128]{2,1,0:T(8,128)S(1)}, s32[]{:T(128)}) %tuple.32), condition=%wide.while_cond, body=%wide.while_body.sunk | while | flops 2 | bytes 131189 | solution.py:14
  198.3 1.4 bitcast_dynamic-update-slice_fusion.2
  200.3 1.4 bitcast_dynamic-update-slice_fusion.2
  202.3 1.4 bitcast_dynamic-update-slice_fusion.2
  204.3 1.4 bitcast_dynamic-update-slice_fusion.2
  205.6 39.3 %custom-call.37 = f32[4,128,128]{1,2,0:T(8,128)S(1)} custom-call(f32[4,128,128]{2,1,0:T(8,128)S(1)} %get-tuple-element.9), custom_call_target="InvertDiagBlocksLowerTriangular" | custom-call | tf_op jit(solution)/shard_map/triangular_solve | solution.py:14
  247.9 1.7 fusion.27
  249.6 2.2 bitcast_convert_fusion
  251.8 1.8 convolution_subtract_fusion.1
  254.7 3.6 %convolution_subtract_fusion = f32[128,2048]{0,1:T(8,128)S(1)} fusion(f32[128,2048]{1,0:T(8,128)S(1)} %fusion.52, f32[128,2048]{1,0:T(8,128)S(1)} %fusion.27, f32[512,2048]{0,1:T(8,128)S(1)} %bitcast_convert_fusion, f32[512,512]{1,0:T(8,128)S(1)} %get-tuple-element.83), kind=kOutput, calls=%fused_computation.12 | convolution fusion | flops 806092800 | bytes 4325376 | tf_op jit(solution)/shard_map/triangular_solve | solution.py:14
  258.3 1.1 fusion.54
  259.4 5.5 %fusion.7 = f32[128,2048]{0,1:T(8,128)S(1)} fusion(f32[128,2048]{1,0:T(8,128)S(1)} %fusion.54, f32[128,2048]{1,0:T(8,128)S(1)} %fusion.52, f32[128,2048]{1,0:T(8,128)S(1)} %fusion.27, f32[512,2048]{0,1:T(8,128)S(1)} %bitcast_convert_fusion, f32[512,512]{1,0:T(8,128)S(1)} %get-tuple-element.83), kind=kOutput, calls=%fused_computation.11 | convolution fusion | flops 1209794560 | bytes 5439488 | tf_op jit(solution)/shard_map/triangular_solve | solution.py:14
  266.9 2.3 convolution_bitcast_fusion
  (73 shorter events, 15.5 us)
Async XLA Ops:
  8.0 8.8 %copy-start = (bf16[3,3,3,64,64]{4,3,2,1,0:T(8,128)(2,1)S(1)}, bf16[3,3,3,64,64]{4,3,2,1,0:T(8,128)(2,1)}, u32[]{:S(2)}) copy-start(bf16[3,3,3,64,64]{4,3,2,1,0:T(8,128)(2,1)} %param.8) | copy-start | bytes 663556
  8.0 97.2 %all-reduce.3.cloned.1.call-start = ((), (), s32[]{:S(2)}) async-start(), calls=%async_computation | async-start | bytes 2097152 | tf_op jit(solution)/shard_map/psum | solution.py:66
  10.7 6.1 %copy-start.4 = (f32[64]{0:T(128)S(1)}, f32[64]{0:T(128)}, u32[]{:S(2)}) copy-start(f32[64]{0:T(128)} %param.9) | copy-start | bytes 772
  23.9 2.4 copy-start.5
  26.2 221.7 %all-gather.2.cloned.1.call-start = ((), (), s32[]{:S(2)}) async-start(), calls=%async_computation.1 | async-start | bytes 2162688 | tf_op jit(solution)/shard_map/all_gather | solution.py:63
  105.2 4.0 %copy-start.2 = (f32[512,512]{0,1:T(8,128)S(1)}, f32[512,512]{0,1:T(8,128)}, u32[]{:S(2)}) copy-start(f32[512,512]{0,1:T(8,128)} %all-reduce.3.cloned.1.call-done) | copy-start | bytes 3145732
  109.5 1.0 copy-start.3
  264.9 2.1 copy-start.1
Sparse Core Ops, SparseCore 0:
  26.3 78.8 all-reduce.2
Sparse Core Ops, SparseCore 1:
  29.2 51.1 all-gather.1
where the time goes:
time: 282 us; the launch traced here: 277 us
  other arithmetic  126 us (45%)
  waiting for transfers between devices  56.9 us (20%)
  matrix products  37.3 us (13%)
  blocking collectives  20.2 us (7%)
  between operations  19.3 us (7%)
  local copies, waits for them, and re-layouts  17.4 us (6%)
    another operation x14, other arithmetic, on_device(): lower = jnp.linalg.cholesky(precision_matrix)  78.9 us
    psum x1, waiting for transfers between devices, on_device(): gram_whole, moment_whole = lax.psum((gram_part, moment), 'mem')  56.9 us
    another operation x3, other arithmetic, tri_solve(): lax.linalg.triangular_solve(lower, rhs, left_side=True, lower=True, trans...  39.4 us
    psum x1, blocking collectives, on_device(): gram_whole, moment_whole = lax.psum((gram_part, moment), 'mem')  20.2 us
    another operation x21, matrix products, tri_solve(): lax.linalg.triangular_solve(lower, rhs, left_side=True, lower=True, trans...  18.8 us
    another operation x12, local copies, waits for them, and re-layouts  7.81 us
    conv_general_dilated x1, matrix products, features_of(): lax.conv_general_dilated(shaped, conv_weight, (1, 1, 1), 'VALID', dimensi...  7.13 us
    unnamed x13, local copies, waits for them, and re-layouts  7.05 us
  transfers between devices with their start and end apart: 2, of which 1 were waited for; matrix products, arithmetic and copies ran while one was open for 51% of the time, Pallas kernels for 0%

commit v1 on v0

v1 whole, which is shorter than its diff:
```python
import functools

import jax
import jax.numpy as jnp
from jax import lax
from jax.experimental import pallas as pl
from jax.experimental.pallas import tpu as pltpu
from jax.sharding import PartitionSpec as P

C = 64
EDGE = 6
NP = 128
HIT = 32
F = 512
NQ = 64
FU = F + 128
PAY = 2 * F + 128
MESH = pl.DeviceIdType.MESH
F32 = jnp.float32
BF16 = jnp.bfloat16
HIGHEST = lax.Precision.HIGHEST


def iota(shape, dim):
    return lax.broadcasted_iota(jnp.int32, shape, dim)


def split2(x):
    hi = x.astype(BF16)
    return hi, (x - hi.astype(F32)).astype(BF16)


def dot(a, b, ca=1, cb=0, precision=None):
    return lax.dot_general(
        a, b, (((ca,), (cb,)), ((), ())), precision=precision, preferred_element_type=F32
    )


def banded(conv_weight):
    parts = [
        jnp.pad(conv_weight, ((0, 0), (0, 0), (zo, 3 - zo), (0, 0), (0, 0))) for zo in (0, 2, 1, 3)
    ]
    return jnp.stack(parts, axis=4).reshape(3, 3 * EDGE * C, 4 * C)


def feature_kernel(count, vox, band, bias, ids, targets, qids, pay, qrows, slab, feats, sem):
    copies = [pltpu.make_async_copy(vox.at[x], slab.at[x], sem.at[x]) for x in range(EDGE)]
    for copy in copies:
        copy.start()

    live = iota((HIT, ids.shape[1]), 1) < count[0]
    mine = jnp.logical_and(ids[...] == iota((HIT, ids.shape[1]), 0), live)
    hits = jnp.sum(jnp.where(mine, 1.0, 0.0), axis=1, keepdims=True)
    tsum = jnp.sum(jnp.where(mine, targets[...], 0.0), axis=1, keepdims=True)
    root = jnp.sqrt(hits)
    scaled = jnp.where(hits > 0, tsum / jnp.where(hits > 0, root, 1.0), 0.0)

    waited = 0
    for cx in range(2):
        acc = None
        for dx in range(3):
            while waited < 2 * cx + dx + 2:
                copies[waited].wait()
                waited += 1
            lhs = jnp.concatenate(
                [
                    slab[2 * cx + dx : 2 * cx + dx + 2, dy : dy + 4].reshape(8 * NP, EDGE * C)
                    for dy in range(3)
                ],
                axis=1,
            )
            part = dot(lhs, band[dx])
            acc = part if acc is None else acc + part
        act = jnp.tanh(acc + bias[...]).reshape(2, 2, 2, NP, 4 * C)
        pooled = act[0, :, 0] + act[0, :, 1] + act[1, :, 0] + act[1, :, 1]
        for cy in range(2):
            cell = (pooled[cy, :, : 2 * C] + pooled[cy, :, 2 * C :]) * 0.125
            feats[:, (2 * cx + cy) * 2 * C : (2 * cx + cy + 1) * 2 * C] = cell

    hi, lo = split2(feats[:HIT, :] * root)
    pay[:, :F] = hi
    pay[:, F : 2 * F] = lo
    t1, t2 = split2(scaled)
    t3 = (scaled - t1.astype(F32) - t2.astype(F32)).astype(BF16)
    lane = iota((HIT, 128), 1)
    tail = jnp.where(lane == 0, t1.astype(F32), 0.0)
    tail = jnp.where(lane == 1, t2.astype(F32), tail)
    tail = jnp.where(lane == 2, t3.astype(F32), tail)
    pay[:, 2 * F :] = tail.astype(BF16)
    pick = (iota((NP, NQ), 0) == qids[...]).astype(F32).astype(BF16)
    qrows[...] = dot(pick, feats[...].astype(BF16), 0, 0).astype(BF16)


def features(vox, band, bias, count, ids, targets, qids):
    vmem = pl.BlockSpec(memory_space=pltpu.VMEM)
    return pl.pallas_call(
        feature_kernel,
        out_shape=(
            jax.ShapeDtypeStruct((HIT, PAY), BF16),
            jax.ShapeDtypeStruct((NQ, F), BF16),
        ),
        in_specs=[
            pl.BlockSpec(memory_space=pltpu.SMEM),
            pl.BlockSpec(memory_space=pl.ANY),
            vmem,
            vmem,
            vmem,
            vmem,
            vmem,
        ],
        out_specs=(vmem, vmem),
        scratch_shapes=[
            pltpu.VMEM((EDGE, EDGE, NP, EDGE * C), BF16),
            pltpu.VMEM((NP, F), F32),
            pltpu.SemaphoreType.DMA((EDGE,)),
        ],
        compiler_params=pltpu.CompilerParams(vmem_limit_bytes=48 << 20),
        name="features",
    )(count, vox, band, bias, ids, targets, qids)


def spread(x, shape=(8, 128)):
    return jnp.broadcast_to(x, shape)


def inverse_factor(gram):
    n = HIT
    wide = jnp.concatenate(
        [gram, jnp.where(iota((n, n), 0) == iota((n, n), 1), 1.0, 0.0), jnp.zeros((n, 64), F32)],
        axis=1,
    )
    sub = iota((8, 128), 0)
    rows = [wide[8 * b : 8 * b + 8] for b in range(4)]
    done = []
    for b in range(4):
        cols = [[spread(rows[t][:, 8 * b + c : 8 * b + c + 1]) for c in range(8)] for t in range(b, 4)]
        for j in range(8):
            heads = [spread(cols[0][c][j : j + 1, :]) for c in range(j, 8)]
            inv = 1.0 / heads[0]
            row = spread(rows[b][j : j + 1, :]) * inv
            heads = [h * inv for h in heads]
            for t in range(4 - b):
                below = jnp.where(sub > j, cols[0][j], 0.0) if t == 0 else cols[t][j]
                rows[b + t] = rows[b + t] - below * row
                for c in range(j + 1, 8):
                    cols[t][c] = cols[t][c] - below * heads[c - j]
        diag = cols[0][0]
        for j in range(1, 8):
            diag = jnp.where(sub == j, cols[0][j], diag)
        done.append(rows[b] * lax.rsqrt(diag))
    return jnp.concatenate(done, axis=0)[:, n : 2 * n]


def group_kernel(
    n_mem, pay, qrows, var, mean,
    blocks, queries, t_hi, t_lo, tt_hi, tt_lo, tt_row,
    bsend, brecv, qloc, xsend, xrecv, ysend, yrecv, csend, crecv,
):
    g, m = lax.axis_index("grp"), lax.axis_index("mem")
    core, plane = lax.rem(g, 2), lax.div(g, 2)
    px, py = lax.rem(plane, 4), lax.div(plane, 4)
    right, left = lax.rem(m + 1, n_mem), lax.rem(m + n_mem - 1, n_mem)
    xs = [(py * 4 + lax.rem(px + s, 4)) * 2 + core for s in (1, 2, 3)]
    ys = [(lax.rem(py + s, 4) * 4 + px) * 2 + core for s in (1, 2, 3)]
    other = plane * 2 + (1 - core)

    barrier = pltpu.get_barrier_semaphore()
    for peer in [(g, right), (g, left)] + [(h, m) for h in xs + ys + [other]]:
        pl.semaphore_signal(barrier, inc=1, device_id=peer, device_id_type=MESH)
    pl.semaphore_wait(barrier, 9)

    def remote(src, dst, send, recv, peer):
        return pltpu.make_async_remote_copy(
            src_ref=src, dst_ref=dst, send_sem=send, recv_sem=recv, device_id=peer, device_id_type=MESH
        )

    def pass_on(slot):
        peer = right if slot % 2 else left
        return remote(
            blocks.at[slot], blocks.at[slot + 2], bsend.at[slot + 2], brecv.at[slot + 2], (g, peer)
        )

    hops = {
        1: remote(pay, blocks.at[1], bsend.at[1], brecv.at[1], (g, right)),
        2: remote(pay, blocks.at[2], bsend.at[2], brecv.at[2], (g, left)),
    }
    for slot in (1, 2, 3, 4, 5):
        hops[slot + 2] = pass_on(slot)
    hops[1].start()
    hops[2].start()
    own = pltpu.make_async_copy(qrows, queries.at[plane, core], qloc.at[0])
    own.start()
    along_x = [
        remote(qrows, queries.at[plane, core], xsend.at[i], xrecv.at[i], (xs[i], m)) for i in range(3)
    ]
    line = queries.at[pl.ds(py * 4, 4), core]
    along_y = [remote(line, line, ysend.at[i], yrecv.at[i], (ys[i], m)) for i in range(3)]
    half = queries.at[:, core]
    across = remote(half, half, csend.at[0], crecv.at[0], (other, m))
    for copy in along_x:
        copy.start()

    t_hi[...] = jnp.zeros_like(t_hi)
    t_lo[...] = jnp.zeros_like(t_lo)
    tt_hi[...] = jnp.zeros_like(tt_hi)
    tt_lo[...] = jnp.zeros_like(tt_lo)

    def eliminate(k):
        src = pay if k == 0 else blocks.at[k]
        a_hi, a_lo = src[:, :F], src[:, F : 2 * F]
        tail = src[:, 2 * F :].astype(F32)
        target = tail[:, 0:1] + tail[:, 1:2] + tail[:, 2:3]
        lane = iota((HIT, 128), 1)
        rest = jnp.concatenate(
            [a_hi.astype(F32) + a_lo.astype(F32), jnp.where(lane == 0, target, 0.0)], axis=1
        )
        both = jnp.concatenate([a_hi, a_lo], axis=0)
        gg = dot(both, both, 1, 1)
        gram = gg[:HIT, :HIT] + (gg[:HIT, HIT:] + gg[HIT:, :HIT])
        gram = gram + jnp.where(iota((HIT, HIT), 0) == iota((HIT, HIT), 1), 8.0, 0.0)
        if k > 0:
            width = 128 * ((32 * k + 127) // 128)
            first = dot(both, tt_hi[:F, :width])
            low = first[:HIT] + (first[HIT:] + dot(a_hi, tt_lo[:F, :width]))
            gram = gram - dot(low, low, 1, 1, HIGHEST)
            l_hi, l_lo = split2(low)
            second = dot(jnp.concatenate([l_hi, l_lo], axis=0), t_hi[:width, :])
            rest = rest - (second[:HIT] + (second[HIT:] + dot(l_hi, t_lo[:width, :])))
        inv = inverse_factor(gram)
        rows = dot(inv, rest, 1, 0, HIGHEST)
        r_hi, r_lo = split2(rows)
        t_hi[HIT * k : HIT * (k + 1), :] = r_hi
        t_lo[HIT * k : HIT * (k + 1), :] = r_lo
        cols = rows.T
        c_hi, c_lo = split2(cols)
        tt_hi[:, HIT * k : HIT * (k + 1)] = c_hi
        tt_lo[:, HIT * k : HIT * (k + 1)] = c_lo
        tt_row[:, HIT * k : HIT * (k + 1)] = cols[F : F + 8, :]

    eliminate(0)
    hops[1].wait_recv()
    hops[2].wait_recv()
    hops[3].start()
    hops[4].start()
    own.wait()
    for copy in along_x:
        copy.wait_recv()
    for copy in along_y:
        copy.start()
    eliminate(1)
    eliminate(2)
    hops[3].wait_recv()
    hops[4].wait_recv()
    hops[5].start()
    hops[6].start()
    eliminate(3)
    eliminate(4)
    hops[5].wait_recv()
    hops[6].wait_recv()
    hops[7].start()
    eliminate(5)
    eliminate(6)
    for copy in along_y:
        copy.wait_recv()
    across.start()
    hops[7].wait_recv()
    eliminate(7)
    across.wait_recv()

    y = tt_row[0:1, :]

    def evaluate(i, carry):
        x = queries[pl.ds(4 * i, 4)].reshape(4 * 2 * NQ, F)
        t = dot(x, tt_hi[:F, :]) + dot(x, tt_lo[:F, :])
        xf = x.astype(F32)
        t0, t1 = t[:, :128], t[:, 128:]
        sq = xf * xf
        sv = (sq[:, :128] + sq[:, 128:256]) + (sq[:, 256:384] + sq[:, 384:]) - (t0 * t0 + t1 * t1)
        sm = t0 * y[:, :128] + t1 * y[:, 128:]
        vs, ms = [], []
        for b in range(4):
            vs.append(jnp.sum(sv[128 * b : 128 * b + 128].T, axis=0, keepdims=True))
            ms.append(jnp.sum(sm[128 * b : 128 * b + 128].T, axis=0, keepdims=True))
        var[i] = jnp.concatenate(vs, axis=0)
        mean[i] = jnp.concatenate(ms, axis=0)
        return carry

    lax.fori_loop(0, 4, evaluate, 0)

    for slot in range(1, 8):
        hops[slot].wait_send()
    for copy in along_x + along_y + [across]:
        copy.wait_send()


def group_posterior(n_mem, pay, qrows):
    vmem = pl.BlockSpec(memory_space=pltpu.VMEM)
    dma = pltpu.SemaphoreType.DMA
    out = jax.ShapeDtypeStruct((4, 4, 128), F32)
    return pl.pallas_call(
        functools.partial(group_kernel, n_mem),
        out_shape=(out, out),
        in_specs=[vmem, vmem],
        out_specs=(vmem, vmem),
        scratch_shapes=[
            pltpu.VMEM((n_mem, HIT, PAY), BF16),
            pltpu.VMEM((16, 2, NQ, F), BF16),
            pltpu.VMEM((256, FU), BF16),
            pltpu.VMEM((256, FU), BF16),
            pltpu.VMEM((FU, 256), BF16),
            pltpu.VMEM((FU, 256), BF16),
            pltpu.VMEM((8, 256), F32),
            dma((8,)), dma((8,)), dma((1,)), dma((3,)), dma((3,)), dma((3,)), dma((3,)), dma((1,)), dma((1,)),
        ],
        compiler_params=pltpu.CompilerParams(
            collective_id=0, has_side_effects=True, vmem_limit_bytes=48 << 20
        ),
        name="group_posterior",
    )(pay, qrows)


def on_device(n_mem, voxels, conv_weight, conv_bias, row_counts, sample_patch, targets, query_patch):
    band = banded(conv_weight)
    bias = jnp.tile(conv_bias, 4).reshape(1, 4 * C)
    pay, qrows = features(
        voxels.transpose(1, 2, 0, 3),
        band,
        bias,
        row_counts,
        sample_patch.reshape(1, -1),
        targets.reshape(1, -1),
        query_patch.reshape(1, -1),
    )
    var, mean = group_posterior(n_mem, pay, qrows)
    return var.reshape(1, 1, -1), mean.reshape(1, 1, -1)


def solution(mesh):
    rows = ("grp", "mem")
    in_specs = (P(rows, None, None, None), P(), P(), P(rows), P(rows), P(rows), P(rows))
    out_specs = (P("grp", "mem", None), P("grp", "mem", None))
    return jax.shard_map(
        functools.partial(on_device, mesh.shape["mem"]),
        mesh=mesh,
        in_specs=in_specs,
        out_specs=out_specs,
        check_vma=False,
    )
```

time: 282 us -> 63.2 us (0.22)
  the two profiles are of different devices: /device:TPU:2 before, /device:TPU:1 now
where the time goes in v1:
time: 63.2 us; the launch traced here: 63 us
  Pallas kernels  42.3 us (67%)
  local copies, waits for them, and re-layouts  18.3 us (29%)
  between operations  1.36 us (2%)
  other arithmetic  0.97 us (2%)
    pallas_call x1, Pallas kernels, group_posterior(): pl.pallas_call(functools.partial(group_kernel, n_mem), out_shape=(out, ou...  32.5 us
    pallas_call x1, Pallas kernels, features(): pl.pallas_call(feature_kernel, out_shape=(jax.ShapeDtypeStruct((HIT, PAY)...  9.79 us
    another operation x2, local copies, waits for them, and re-layouts, banded(): return jnp.stack(parts, axis=4).reshape(3, 3 * EDGE * C, 4 * C)  9.65 us
    reshape x1, local copies, waits for them, and re-layouts, banded(): return jnp.stack(parts, axis=4).reshape(3, 3 * EDGE * C, 4 * C)  5.39 us
    unnamed x12, local copies, waits for them, and re-layouts  3.21 us

profile of v1, /device:TPU:1, one launch (start us, length us, event | category | flops | bytes accessed | tf_op | source)
XLA Modules:
  0.0 63.0 jit_solution(13104126154290251360)
XLA Ops:
  0.6 2.7 %pad_bitcast_fusion.3 = (bf16[3,3,6,64,1,64]{5,3,2,1,0,4:T(8,128)(2,1)S(1)}, bf16[3,3,6,64,1,64]{5,3,2,1,0,4:T(8,128)(2,1)S(1)}, bf16[3,3,6,64,1,64]{5,3,2,1,0,4:T(8,128)(2,1)S(1)}, bf16[3,3,6,64,1,64]{5,3,2,1,0,4:T(8,128)(2,1)S(1)}) fusion(bf16[3,3,3,64,64]{4,3,2,1,0:T(8,128)(2,1)} %param.8), kind=kLoop, calls=%fused_computation.4 | loop fusion | bytes 1990656 | tf_op jit(solution)/shard_map/stack | solution.py:43
  3.4 1.0 %pad_maximum_fusion = bf16[3,3,6,64,4,64]{5,3,2,1,0,4:T(8,128)(2,1)S(1)} fusion(bf16[3,3,6,64,1,64]{5,3,2,1,0,4:T(8,128)(2,1)S(1)} %get-tuple-element.12, bf16[3,3,6,64,1,64]{5,3,2,1,0,4:T(8,128)(2,1)S(1)} %get-tuple-element.13, bf16[3,3,6,64,1,64]{5,3,2,1,0,4:T(8,128)(2,1)S(1)} %get-tuple-element.11, bf16[3,3,6,64,1,64]{5,3,2,1,0,4:T(8,128)(2,1)S(1)} %get-tuple-element.10), kind=kLoop, calls=%fused_computation | loop fusion | flops 2654208 | bytes 3538944 | tf_op jit(solution)/shard_map/stack | solution.py:43
  4.3 6.9 %copy.9 = bf16[3,3,6,64,4,64]{5,4,3,2,1,0:T(4,128)(2,1)} copy(bf16[3,3,6,64,4,64]{5,3,2,1,0,4:T(8,128)(2,1)S(1)} %pad_maximum_fusion) | data formatting | bytes 3538944 | tf_op jit(solution)/shard_map/stack | solution.py:43
  11.3 0.0 copy-start.4
  11.3 0.0 copy-start.1
  11.3 0.0 copy-start.2
  11.3 0.0 copy-start.3
  11.3 5.4 %reshape.23.band = bf16[3,1152,256]{2,1,0:T(8,128)(2,1)S(1)} reshape(bf16[3,3,6,64,4,64]{5,4,3,2,1,0:T(4,128)(2,1)} %copy.9) | data formatting | bytes 3538944 | tf_op jit(solution)/shard_map/reshape | solution.py:43
  16.7 0.0 copy-done.4
  16.7 0.1 reshape_tile.3.bias
  17.4 0.0 copy-done.1
  17.4 0.0 copy-done.2
  17.4 0.0 copy-done.3
  17.4 0.0 copy-start
  17.5 2.0 %copy-done = bf16[128,6,6,384]{3,0,2,1:T(8,128)(2,1)S(1)} copy-done((bf16[128,6,6,384]{3,0,2,1:T(8,128)(2,1)S(1)}, bf16[128,6,6,384]{3,0,2,1:T(8,128)(2,1)}, u32[]{:S(2)}) %copy-start) | copy-done | bytes 3538968
  19.5 9.8 %features.1 = (bf16[32,1152]{1,0:T(8,128)(2,1)S(1)}, bf16[64,512]{1,0:T(8,128)(2,1)S(1)}) custom-call(s32[1]{0:T(128)S(6)} %copy.12.count, bf16[6,6,128,384]{3,2,1,0:T(8,128)(2,1)S(1)} %bitcast.14, bf16[3,1152,256]{2,1,0:T(8,128)(2,1)S(1)} %reshape.23.band, f32[1,256]{1,0:T(1,128)S(1)} %reshape_tile.3.bias, s32[1,2048]{1,0:T(1,128)S(1)} %bitcast.15, ...), custom_call_target="tpu_custom_call" | custom-call | tf_op jit(solution)/shard_map/features/pallas_call | solution.py:96
  29.3 32.5 %group_posterior.1 = (f32[4,4,128]{2,1,0:T(4,128)S(1)}, f32[4,4,128]{2,1,0:T(4,128)S(1)}) custom-call(bf16[32,1152]{1,0:T(8,128)(2,1)S(1)} %get-tuple-element.6.pay, bf16[64,512]{1,0:T(8,128)(2,1)S(1)} %get-tuple-element.7.qrows), custom_call_target="tpu_custom_call" | custom-call | tf_op jit(solution)/shard_map/group_posterior/pallas_call | solution.py:300
  61.8 0.6 copy.13
  62.4 0.6 copy.14
  (1 shorter events, 0.0 us)
Async XLA Ops:
  11.3 5.4 %copy-start.4 = (f32[64]{0:T(128)S(1)}, f32[64]{0:T(128)}, u32[]{:S(2)}) copy-start(f32[64]{0:T(128)} %param.9) | copy-start | bytes 772
  11.3 6.2 %copy-start.1 = (s32[2048]{0:T(1024)S(1)}, s32[2048]{0:T(1024)}, u32[]{:S(2)}) copy-start(s32[2048]{0:T(1024)} %param.11) | copy-start | bytes 24580
  11.3 6.2 %copy-start.2 = (f32[2048]{0:T(1024)S(1)}, f32[2048]{0:T(1024)}, u32[]{:S(2)}) copy-start(f32[2048]{0:T(1024)} %param.12) | copy-start | bytes 24580
  11.3 6.2 %copy-start.3 = (s32[64]{0:T(128)S(1)}, s32[64]{0:T(128)}, u32[]{:S(2)}) copy-start(s32[64]{0:T(128)} %param.13) | copy-start | bytes 772
  17.4 2.0 %copy-start = (bf16[128,6,6,384]{3,0,2,1:T(8,128)(2,1)S(1)}, bf16[128,6,6,384]{3,0,2,1:T(8,128)(2,1)}, u32[]{:S(2)}) copy-start(bf16[128,6,6,384]{3,0,2,1:T(8,128)(2,1)} %param.7) | copy-start | bytes 10616836

commit v2 on v1

v2 whole, which is shorter than its diff:
```python
import functools

import jax
import jax.numpy as jnp
from jax import lax
from jax.experimental import pallas as pl
from jax.experimental.pallas import tpu as pltpu
from jax.sharding import PartitionSpec as P

C = 64
EDGE = 6
NP = 128
HIT = 32
F = 512
NQ = 64
FU = F + 128
PAY = 2 * F + 128
MESH = pl.DeviceIdType.MESH
F32 = jnp.float32
BF16 = jnp.bfloat16
HIGHEST = lax.Precision.HIGHEST


def iota(shape, dim):
    return lax.broadcasted_iota(jnp.int32, shape, dim)


def split2(x):
    hi = x.astype(BF16)
    return hi, (x - hi.astype(F32)).astype(BF16)


def dot(a, b, ca=1, cb=0, precision=None):
    return lax.dot_general(
        a, b, (((ca,), (cb,)), ((), ())), precision=precision, preferred_element_type=F32
    )


def fill_band(weight, band):
    zero = jnp.zeros((C, C), BF16)
    for dx in range(3):
        for dy in range(3):
            taps = [weight[dx, dy, dz] for dz in range(3)]
            at = lambda d: taps[d] if 0 <= d <= 2 else zero
            for zi in range(EDGE):
                row = (dx * 3 + dy) * EDGE * C + zi * C
                band[row : row + C, : 2 * C] = jnp.concatenate([at(zi), at(zi - 2)], axis=1)
                band[row : row + C, 2 * C :] = jnp.concatenate([at(zi - 1), at(zi - 3)], axis=1)


def feature_kernel(
    count, vox, weight, bias, ids, targets, qids, pay, qrows, slab, taps, band, feats, sem, wsem
):
    copies = [pltpu.make_async_copy(vox.at[x], slab.at[x], sem.at[x]) for x in range(EDGE)]
    taps_in = pltpu.make_async_copy(weight, taps, wsem.at[0])
    taps_in.start()
    for copy in copies:
        copy.start()

    live = iota((HIT, ids.shape[1]), 1) < count[0]
    mine = jnp.logical_and(ids[...] == iota((HIT, ids.shape[1]), 0), live)
    hits = jnp.sum(jnp.where(mine, 1.0, 0.0), axis=1, keepdims=True)
    tsum = jnp.sum(jnp.where(mine, targets[...], 0.0), axis=1, keepdims=True)
    root = jnp.sqrt(hits)
    scaled = jnp.where(hits > 0, tsum / jnp.where(hits > 0, root, 1.0), 0.0)
    t1, t2 = split2(scaled)
    t3 = (scaled - t1.astype(F32) - t2.astype(F32)).astype(BF16)
    lane = iota((HIT, 128), 1)
    tail = jnp.where(lane == 0, t1.astype(F32), 0.0)
    tail = jnp.where(lane == 1, t2.astype(F32), tail)
    tail = jnp.where(lane == 2, t3.astype(F32), tail)
    pay[:, 2 * F :] = tail.astype(BF16)

    taps_in.wait()
    fill_band(taps, band)
    shift = jnp.concatenate([bias[...]] * 4, axis=1)
    waited = 0
    for cx in range(2):
        while waited < 2 * cx + 4:
            copies[waited].wait()
            waited += 1
        for cy in range(2):
            lhs = jnp.concatenate(
                [
                    slab[2 * cx + dx : 2 * cx + dx + 2, 2 * cy + dy : 2 * cy + dy + 2].reshape(
                        4 * NP, EDGE * C
                    )
                    for dx in range(3)
                    for dy in range(3)
                ],
                axis=1,
            )
            act = jnp.tanh(dot(lhs, band[...]) + shift).reshape(4, NP, 4 * C)
            pooled = (act[0] + act[1]) + (act[2] + act[3])
            cell = (pooled[:, : 2 * C] + pooled[:, 2 * C :]) * 0.125
            feats[:, (2 * cx + cy) * 2 * C : (2 * cx + cy + 1) * 2 * C] = cell

    hi, lo = split2(feats[:HIT, :] * root)
    pay[:, :F] = hi
    pay[:, F : 2 * F] = lo
    pick = (iota((NP, NQ), 0) == qids[...]).astype(F32).astype(BF16)
    qrows[...] = dot(pick, feats[...].astype(BF16), 0, 0).astype(BF16)


def features(vox, weight, bias, count, ids, targets, qids):
    vmem, hbm = pl.BlockSpec(memory_space=pltpu.VMEM), pl.BlockSpec(memory_space=pl.ANY)
    return pl.pallas_call(
        feature_kernel,
        out_shape=(
            jax.ShapeDtypeStruct((HIT, PAY), BF16),
            jax.ShapeDtypeStruct((NQ, F), BF16),
        ),
        in_specs=[pl.BlockSpec(memory_space=pltpu.SMEM), hbm, hbm, vmem, vmem, vmem, vmem],
        out_specs=(vmem, vmem),
        scratch_shapes=[
            pltpu.VMEM((EDGE, EDGE, NP, EDGE * C), BF16),
            pltpu.VMEM((3, 3, 3, C, C), BF16),
            pltpu.VMEM((9 * EDGE * C, 4 * C), BF16),
            pltpu.VMEM((NP, F), F32),
            pltpu.SemaphoreType.DMA((EDGE,)),
            pltpu.SemaphoreType.DMA((1,)),
        ],
        compiler_params=pltpu.CompilerParams(vmem_limit_bytes=56 << 20),
        name="features",
    )(count, vox, weight, bias, ids, targets, qids)


def spread(x, shape=(8, 128)):
    return jnp.broadcast_to(x, shape)


def inverse_factor(gram):
    n = gram.shape[0]
    eye = jnp.where(iota((n, n), 0) == iota((n, n), 1), 1.0, 0.0)
    parts = [gram, eye] if n == 64 else [gram, eye, jnp.zeros((n, 128 - 2 * n), F32)]
    wide = jnp.concatenate(parts, axis=1)
    sub = iota((8, 128), 0)
    count = n // 8
    rows = [wide[8 * b : 8 * b + 8] for b in range(count)]
    done = []
    for b in range(count):
        cols = [
            [spread(rows[t][:, 8 * b + c : 8 * b + c + 1]) for c in range(8)] for t in range(b, count)
        ]
        for j in range(8):
            heads = [spread(cols[0][c][j : j + 1, :]) for c in range(j, 8)]
            inv = 1.0 / heads[0]
            row = spread(rows[b][j : j + 1, :]) * inv
            heads = [h * inv for h in heads]
            for t in range(count - b):
                below = jnp.where(sub > j, cols[0][j], 0.0) if t == 0 else cols[t][j]
                rows[b + t] = rows[b + t] - below * row
                for c in range(j + 1, 8):
                    cols[t][c] = cols[t][c] - below * heads[c - j]
        diag = cols[0][0]
        for j in range(1, 8):
            diag = jnp.where(sub == j, cols[0][j], diag)
        done.append(rows[b] * lax.rsqrt(diag))
    return jnp.concatenate(done, axis=0)[:, n : 2 * n]


def eliminate(src, at, first, t_hi, t_lo, tt_hi, tt_lo, tt_row):
    n = src.shape[0]
    a_hi, a_lo = src[:, :F], src[:, F : 2 * F]
    tail = src[:, 2 * F :].astype(F32)
    target = tail[:, 0:1] + tail[:, 1:2] + tail[:, 2:3]
    rest = jnp.concatenate(
        [a_hi.astype(F32) + a_lo.astype(F32), jnp.where(iota((n, 128), 1) == 0, target, 0.0)], axis=1
    )
    both = jnp.concatenate([a_hi, a_lo], axis=0)
    gg = dot(both, both, 1, 1)
    gram = gg[:n, :n] + (gg[:n, n:] + gg[n:, :n])
    gram = gram + jnp.where(iota((n, n), 0) == iota((n, n), 1), 8.0, 0.0)
    if not first:
        part = dot(both, tt_hi[:F, :])
        low = part[:n] + (part[n:] + dot(a_hi, tt_lo[:F, :]))
        gram = gram - dot(low, low, 1, 1, HIGHEST)
        l_hi, l_lo = split2(low)
        part = dot(jnp.concatenate([l_hi, l_lo], axis=0), t_hi[...])
        rest = rest - (part[:n] + (part[n:] + dot(l_hi, t_lo[...])))
    rows = dot(inverse_factor(gram), rest, 1, 0, HIGHEST)
    r_hi, r_lo = split2(rows)
    t_hi[at : at + n, :] = r_hi
    t_lo[at : at + n, :] = r_lo
    cols = rows.T
    c_hi, c_lo = split2(cols)
    tt_hi[:, at : at + n] = c_hi
    tt_lo[:, at : at + n] = c_lo
    tt_row[:, at : at + n] = cols[F : F + 8, :]


def evaluate(queries, tt_hi, tt_lo, tt_row, out):
    y = tt_row[0:1, :]

    def chunk(i, carry):
        x = queries[pl.ds(4 * i, 4)].reshape(4 * 2 * NQ, F)
        t = dot(x, tt_hi[:F, :]) + dot(x, tt_lo[:F, :])
        xf = x.astype(F32)
        t0, t1 = t[:, :128], t[:, 128:]
        sq = xf * xf
        sv = (sq[:, :128] + sq[:, 128:256]) + (sq[:, 256:384] + sq[:, 384:]) - (t0 * t0 + t1 * t1)
        sm = t0 * y[:, :128] + t1 * y[:, 128:]
        for half, part in ((0, sv), (1, sm)):
            lines = [
                jnp.sum(part[128 * b : 128 * b + 128].T, axis=0, keepdims=True) for b in range(4)
            ]
            out[half, i] = jnp.concatenate(lines, axis=0)
        return carry

    lax.fori_loop(0, 4, chunk, 0)


def group_kernel(
    n_mem, pay, qrows, out,
    blocks, queries, t_hi, t_lo, tt_hi, tt_lo, tt_row,
    bsend, brecv, qloc, psend, precv, lsend, lrecv, csend, crecv,
):
    g, m = lax.axis_index("grp"), lax.axis_index("mem")
    core, plane = lax.rem(g, 2), lax.div(g, 2)
    px, py = lax.rem(plane, 4), lax.div(plane, 4)
    right, left = lax.rem(m + 1, n_mem), lax.rem(m + n_mem - 1, n_mem)
    xs = [(py * 4 + lax.rem(px + s, 4)) * 2 + core for s in (1, 2, 3)]
    ys = [(lax.rem(py + s, 4) * 4 + px) * 2 + core for s in (1, 2, 3)]
    other = plane * 2 + (1 - core)

    barrier = pltpu.get_barrier_semaphore()
    for peer in [(g, right), (g, left)] + [(h, m) for h in xs + ys + [other]]:
        pl.semaphore_signal(barrier, inc=1, device_id=peer, device_id_type=MESH)
    pl.semaphore_wait(barrier, 9)

    def remote(src, dst, send, recv, peer):
        return pltpu.make_async_remote_copy(
            src_ref=src, dst_ref=dst, send_sem=send, recv_sem=recv, device_id=peer, device_id_type=MESH
        )

    def pass_on(slot):
        peer = right if slot % 2 else left
        return remote(
            blocks.at[slot], blocks.at[slot + 2], bsend.at[slot + 2], brecv.at[slot + 2], (g, peer)
        )

    hops = {
        1: remote(pay, blocks.at[1], bsend.at[1], brecv.at[1], (g, right)),
        2: remote(pay, blocks.at[2], bsend.at[2], brecv.at[2], (g, left)),
    }
    for slot in (1, 2, 3, 4, 5):
        hops[slot + 2] = pass_on(slot)
    hops[1].start()
    hops[2].start()
    base = pltpu.make_async_copy(pay, blocks.at[0], qloc.at[1])
    base.start()

    half = NQ // 2
    top, bottom = pl.ds(0, half), pl.ds(half, half)
    near = [
        remote(qrows.at[top], queries.at[py, px, core, top], psend.at[i], precv.at[i], (xs[i], m))
        for i in range(3)
    ] + [
        remote(
            qrows.at[bottom], queries.at[py, px, core, bottom], psend.at[3 + i], precv.at[3 + i], (ys[i], m)
        )
        for i in range(3)
    ]
    row, column = queries.at[py, :, core, top], queries.at[:, px, core, bottom]
    far = [remote(row, row, lsend.at[i], lrecv.at[i], (ys[i], m)) for i in range(3)] + [
        remote(column, column, lsend.at[3 + i], lrecv.at[3 + i], (xs[i], m)) for i in range(3)
    ]
    mine = queries.at[:, :, core]
    across = remote(mine, mine, csend.at[0], crecv.at[0], (other, m))
    own = pltpu.make_async_copy(qrows, queries.at[py, px, core], qloc.at[0])
    for copy in near:
        copy.start()
    own.start()

    factor = (t_hi, t_lo, tt_hi, tt_lo, tt_row)
    for ref in factor:
        ref[...] = jnp.zeros_like(ref)

    base.wait()
    eliminate(blocks[0], 192, True, *factor)
    hops[1].wait_recv()
    hops[2].wait_recv()
    hops[3].start()
    hops[4].start()
    own.wait()
    for copy in near:
        copy.wait_recv()
    for copy in far:
        copy.start()
    eliminate(blocks[1:3].reshape(2 * HIT, PAY), 0, False, *factor)
    hops[3].wait_recv()
    hops[4].wait_recv()
    hops[5].start()
    hops[6].start()
    eliminate(blocks[3:5].reshape(2 * HIT, PAY), 64, False, *factor)
    hops[5].wait_recv()
    hops[6].wait_recv()
    hops[7].start()
    eliminate(blocks[5:7].reshape(2 * HIT, PAY), 128, False, *factor)
    for copy in far:
        copy.wait_recv()
    across.start()
    hops[7].wait_recv()
    eliminate(blocks[7], 224, False, *factor)
    across.wait_recv()
    evaluate(queries.reshape(16, 2, NQ, F), tt_hi, tt_lo, tt_row, out)

    for slot in range(1, 8):
        hops[slot].wait_send()
    for copy in near + far + [across]:
        copy.wait_send()


def group_posterior(n_mem, pay, qrows):
    vmem = pl.BlockSpec(memory_space=pltpu.VMEM)
    dma = pltpu.SemaphoreType.DMA
    return pl.pallas_call(
        functools.partial(group_kernel, n_mem),
        out_shape=jax.ShapeDtypeStruct((2, 4, 4, 128), F32),
        in_specs=[pl.BlockSpec(memory_space=pl.ANY)] * 2,
        out_specs=vmem,
        scratch_shapes=[
            pltpu.VMEM((n_mem, HIT, PAY), BF16),
            pltpu.VMEM((4, 4, 2, NQ, F), BF16),
            pltpu.VMEM((256, FU), BF16),
            pltpu.VMEM((256, FU), BF16),
            pltpu.VMEM((FU, 256), BF16),
            pltpu.VMEM((FU, 256), BF16),
            pltpu.VMEM((8, 256), F32),
            dma((8,)), dma((8,)), dma((2,)), dma((6,)), dma((6,)), dma((6,)), dma((6,)), dma((1,)), dma((1,)),
        ],
        compiler_params=pltpu.CompilerParams(
            collective_id=0, has_side_effects=True, vmem_limit_bytes=48 << 20
        ),
        name="group_posterior",
    )(pay, qrows)


def on_device(n_mem, voxels, conv_weight, conv_bias, row_counts, sample_patch, targets, query_patch):
    pay, qrows = features(
        voxels.transpose(1, 2, 0, 3),
        conv_weight,
        conv_bias.reshape(1, C),
        row_counts,
        sample_patch.reshape(1, -1),
        targets.reshape(1, -1),
        query_patch.reshape(1, -1),
    )
    out = group_posterior(n_mem, pay, qrows)
    return out[0].reshape(1, 1, -1), out[1].reshape(1, 1, -1)


def solution(mesh):
    rows = ("grp", "mem")
    in_specs = (P(rows, None, None, None), P(), P(), P(rows), P(rows), P(rows), P(rows))
    out_specs = (P("grp", "mem", None), P("grp", "mem", None))
    return jax.shard_map(
        functools.partial(on_device, mesh.shape["mem"]),
        mesh=mesh,
        in_specs=in_specs,
        out_specs=out_specs,
        check_vma=False,
    )
```

time: 63.2 us -> 40.6 us (0.64)
  local copies, waits for them, and re-layouts: 18.3 us -> 2.32 us
  Pallas kernels: 42.3 us -> 36.7 us
  other arithmetic: 0.97 us -> 0 us
    another operation x4 -> x0, local copies, waits for them, and re-layouts: 9.74 us -> none  [the longest x2 9.65 us: banded(): return jnp.stack(parts, axis=4).reshape(3, 3 * EDGE * C, 4 * C)]
    reshape x1 -> x0, local copies, waits for them, and re-layouts: 5.39 us -> none  [banded(): return jnp.stack(parts, axis=4).reshape(3, 3 * EDGE * C, 4 * C)]
    pallas_call x1, Pallas kernels: 32.5 us -> 28.9 us  [group_posterior(): pl.pallas_call(functools.partial(group_kernel, n_mem), out_shape=jax.Shap...]
    pallas_call x1, Pallas kernels: 9.79 us -> 7.85 us  [features(): pl.pallas_call(feature_kernel, out_shape=(jax.ShapeDtypeStruct((HIT, PAY)...]
    unnamed x12 -> x4, local copies, waits for them, and re-layouts: 3.21 us -> 1.72 us
    another operation x1 -> x0, other arithmetic: 0.97 us -> none  [banded(): return jnp.stack(parts, axis=4).reshape(3, 3 * EDGE * C, 4 * C)]
where the time goes in v2:
time: 40.6 us; the launch traced here: 40.4 us
  Pallas kernels  36.7 us (90%)
  local copies, waits for them, and re-layouts  2.32 us (6%)
  between operations  1.3 us (3%)
    pallas_call x1, Pallas kernels, group_posterior(): pl.pallas_call(functools.partial(group_kernel, n_mem), out_shape=jax.Shap...  28.9 us
    pallas_call x1, Pallas kernels, features(): pl.pallas_call(feature_kernel, out_shape=(jax.ShapeDtypeStruct((HIT, PAY)...  7.85 us
    unnamed x4, local copies, waits for them, and re-layouts  1.72 us

profile of v2, /device:TPU:1, one launch (start us, length us, event | category | flops | bytes accessed | tf_op | source)
XLA Modules:
  0.0 40.4 jit_solution(18367287697122146990)
XLA Ops:
  1.3 7.9 %features.1 = (bf16[32,1152]{1,0:T(8,128)(2,1)}, bf16[64,512]{1,0:T(8,128)(2,1)}) custom-call(s32[1]{0:T(128)S(6)} %copy.9.count, bf16[6,6,128,384]{3,2,1,0:T(8,128)(2,1)} %bitcast.7, bf16[3,3,3,64,64]{4,3,2,1,0:T(8,128)(2,1)} %weight.1, f32[1,64]{1,0:T(1,128)} %bitcast.12, s32[1,2048]{1,0:T(1,128)} %bitcast.8, f32[1,2048]{1,0:T(1,128)} %bitcast.9, ...), custom_call_target="tpu_custom_call" | custom-call | tf_op jit(solution)/shard_map/features/pallas_call | solution.py:107
  9.1 0.0 copy-start
  9.1 0.9 %copy-done = bf16[32,1152]{1,0:T(8,128)(2,1)S(1)} copy-done((bf16[32,1152]{1,0:T(8,128)(2,1)S(1)}, bf16[32,1152]{1,0:T(8,128)(2,1)}, u32[]{:S(2)}) %copy-start) | copy-done | bytes 73752
  10.0 0.0 copy-start.1
  10.0 0.8 %copy-done.1 = bf16[64,512]{1,0:T(8,128)(2,1)S(1)} copy-done((bf16[64,512]{1,0:T(8,128)(2,1)S(1)}, bf16[64,512]{1,0:T(8,128)(2,1)}, u32[]{:S(2)}) %copy-start.1) | copy-done | bytes 65560
  10.9 28.9 %group_posterior.1 = f32[2,4,4,128]{3,2,1,0:T(4,128)S(1)} custom-call(bf16[32,1152]{1,0:T(8,128)(2,1)S(1)} %copy-done, bf16[64,512]{1,0:T(8,128)(2,1)S(1)} %copy-done.1), custom_call_target="tpu_custom_call" | custom-call | tf_op jit(solution)/shard_map/group_posterior/pallas_call | solution.py:317
  39.8 0.6 %fusion = (f32[1,4,4,128]{3,2,1,0:T(4,128)}, f32[1,4,4,128]{3,2,1,0:T(4,128)}) fusion(f32[2,4,4,128]{3,2,1,0:T(4,128)S(1)} %group_posterior.1), kind=kLoop, calls=%fused_computation | loop fusion | bytes 32768 | tf_op jit(solution)/shard_map/slice | solution.py:350
Async XLA Ops:
  9.1 0.9 %copy-start = (bf16[32,1152]{1,0:T(8,128)(2,1)S(1)}, bf16[32,1152]{1,0:T(8,128)(2,1)}, u32[]{:S(2)}) copy-start(bf16[32,1152]{1,0:T(8,128)(2,1)} %get-tuple-element.4.pay) | copy-start | bytes 221188
  10.0 0.8 %copy-start.1 = (bf16[64,512]{1,0:T(8,128)(2,1)S(1)}, bf16[64,512]{1,0:T(8,128)(2,1)}, u32[]{:S(2)}) copy-start(bf16[64,512]{1,0:T(8,128)(2,1)} %get-tuple-element.5.qrows) | copy-start | bytes 196612

commit v3 on v2

--- a/solution.py
+++ b/solution.py
@@ -14,7 +14,7 @@
 F = 512
 NQ = 64
 FU = F + 128
-PAY = 2 * F + 128
+TOP = 32767.0
 MESH = pl.DeviceIdType.MESH
 F32 = jnp.float32
 BF16 = jnp.bfloat16
@@ -49,7 +49,7 @@
 
 
 def feature_kernel(
-    count, vox, weight, bias, ids, targets, qids, pay, qrows, slab, taps, band, feats, sem, wsem
+    count, vox, weight, bias, ids, targets, qids, pay, aux, qrows, slab, taps, band, feats, sem, wsem
 ):
     copies = [pltpu.make_async_copy(vox.at[x], slab.at[x], sem.at[x]) for x in range(EDGE)]
     taps_in = pltpu.make_async_copy(weight, taps, wsem.at[0])
@@ -63,14 +63,6 @@
     tsum = jnp.sum(jnp.where(mine, targets[...], 0.0), axis=1, keepdims=True)
     root = jnp.sqrt(hits)
     scaled = jnp.where(hits > 0, tsum / jnp.where(hits > 0, root, 1.0), 0.0)
-    t1, t2 = split2(scaled)
-    t3 = (scaled - t1.astype(F32) - t2.astype(F32)).astype(BF16)
-    lane = iota((HIT, 128), 1)
-    tail = jnp.where(lane == 0, t1.astype(F32), 0.0)
-    tail = jnp.where(lane == 1, t2.astype(F32), tail)
-    tail = jnp.where(lane == 2, t3.astype(F32), tail)
-    pay[:, 2 * F :] = tail.astype(BF16)
-
     taps_in.wait()
     fill_band(taps, band)
     shift = jnp.concatenate([bias[...]] * 4, axis=1)
@@ -95,9 +87,14 @@
             cell = (pooled[:, : 2 * C] + pooled[:, 2 * C :]) * 0.125
             feats[:, (2 * cx + cy) * 2 * C : (2 * cx + cy + 1) * 2 * C] = cell
 
-    hi, lo = split2(feats[:HIT, :] * root)
-    pay[:, :F] = hi
-    pay[:, F : 2 * F] = lo
+    rows = feats[:HIT, :]
+    peak = jnp.max(jnp.abs(rows), axis=1, keepdims=True)
+    unit = jnp.where(peak > 0, TOP / jnp.where(peak > 0, peak, 1.0), 0.0)
+    pay[...] = jnp.round(rows * unit).astype(jnp.int32).astype(jnp.int16)
+    lane = iota((HIT, 128), 1)
+    sides = jnp.where(lane == 0, scaled, jnp.where(lane == 1, peak * (root * (1.0 / TOP)), 0.0))
+    aux[...] = jnp.zeros_like(aux)
+    aux[:, :HIT] = sides.T[:8, :]
     pick = (iota((NP, NQ), 0) == qids[...]).astype(F32).astype(BF16)
     qrows[...] = dot(pick, feats[...].astype(BF16), 0, 0).astype(BF16)
 
@@ -107,11 +104,12 @@
     return pl.pallas_call(
         feature_kernel,
         out_shape=(
-            jax.ShapeDtypeStruct((HIT, PAY), BF16),
+            jax.ShapeDtypeStruct((HIT, F), jnp.int16),
+            jax.ShapeDtypeStruct((8, 128), F32),
             jax.ShapeDtypeStruct((NQ, F), BF16),
         ),
         in_specs=[pl.BlockSpec(memory_space=pltpu.SMEM), hbm, hbm, vmem, vmem, vmem, vmem],
-        out_specs=(vmem, vmem),
+        out_specs=(vmem, vmem, vmem),
         scratch_shapes=[
             pltpu.VMEM((EDGE, EDGE, NP, EDGE * C), BF16),
             pltpu.VMEM((3, 3, 3, C, C), BF16),
@@ -159,13 +157,16 @@
     return jnp.concatenate(done, axis=0)[:, n : 2 * n]
 
 
-def eliminate(src, at, first, t_hi, t_lo, tt_hi, tt_lo, tt_row):
-    n = src.shape[0]
-    a_hi, a_lo = src[:, :F], src[:, F : 2 * F]
-    tail = src[:, 2 * F :].astype(F32)
-    target = tail[:, 0:1] + tail[:, 1:2] + tail[:, 2:3]
+def eliminate(codes, sides, at, first, t_hi, t_lo, tt_hi, tt_lo, tt_row):
+    n = codes.shape[0]
+    column = jnp.concatenate([side.T[:HIT] for side in sides], axis=0)
+    a_hi, a_lo = split2(codes.astype(jnp.int32).astype(F32) * column[:, 1:2])
     rest = jnp.concatenate(
-        [a_hi.astype(F32) + a_lo.astype(F32), jnp.where(iota((n, 128), 1) == 0, target, 0.0)], axis=1
+        [
+            a_hi.astype(F32) + a_lo.astype(F32),
+            jnp.where(iota((n, 128), 1) == 0, column[:, 0:1], 0.0),
+        ],
+        axis=1,
     )
     both = jnp.concatenate([a_hi, a_lo], axis=0)
     gg = dot(both, both, 1, 1)
@@ -189,85 +190,80 @@
     tt_row[:, at : at + n] = cols[F : F + 8, :]
 
 
-def evaluate(queries, tt_hi, tt_lo, tt_row, out):
+def evaluate(queries, tt_hi, tt_lo, tt_row):
     y = tt_row[0:1, :]
-
-    def chunk(i, carry):
-        x = queries[pl.ds(4 * i, 4)].reshape(4 * 2 * NQ, F)
+    var, mean = [], []
+    for i in range(2):
+        x = queries[8 * i : 8 * i + 8].reshape(8 * NQ, F)
         t = dot(x, tt_hi[:F, :]) + dot(x, tt_lo[:F, :])
         xf = x.astype(F32)
         t0, t1 = t[:, :128], t[:, 128:]
         sq = xf * xf
         sv = (sq[:, :128] + sq[:, 128:256]) + (sq[:, 256:384] + sq[:, 384:]) - (t0 * t0 + t1 * t1)
         sm = t0 * y[:, :128] + t1 * y[:, 128:]
-        for half, part in ((0, sv), (1, sm)):
-            lines = [
-                jnp.sum(part[128 * b : 128 * b + 128].T, axis=0, keepdims=True) for b in range(4)
-            ]
-            out[half, i] = jnp.concatenate(lines, axis=0)
-        return carry
-
-    lax.fori_loop(0, 4, chunk, 0)
+        for part, lines in ((sv, var), (sm, mean)):
+            for b in range(4):
+                lines.append(jnp.sum(part[128 * b : 128 * b + 128].T, axis=0, keepdims=True))
+    return jnp.concatenate(var, axis=0), jnp.concatenate(mean, axis=0)
 
 
 def group_kernel(
-    n_mem, pay, qrows, out,
-    blocks, queries, t_hi, t_lo, tt_hi, tt_lo, tt_row,
-    bsend, brecv, qloc, psend, precv, lsend, lrecv, csend, crecv,
+    n_mem, pay, aux, qrows, out,
+    blocks, sides, queries, t_hi, t_lo, tt_hi, tt_lo, tt_row,
+    bsend, brecv, ssend, srecv, qloc, psend, precv, lsend, lrecv, csend, crecv,
 ):
     g, m = lax.axis_index("grp"), lax.axis_index("mem")
     core, plane = lax.rem(g, 2), lax.div(g, 2)
     px, py = lax.rem(plane, 4), lax.div(plane, 4)
-    right, left = lax.rem(m + 1, n_mem), lax.rem(m + n_mem - 1, n_mem)
+    zs = [lax.rem(m + n_mem + d, n_mem) for d in (1, -1, 2, -2, 3, -3, 4)]
     xs = [(py * 4 + lax.rem(px + s, 4)) * 2 + core for s in (1, 2, 3)]
     ys = [(lax.rem(py + s, 4) * 4 + px) * 2 + core for s in (1, 2, 3)]
     other = plane * 2 + (1 - core)
 
     barrier = pltpu.get_barrier_semaphore()
-    for peer in [(g, right), (g, left)] + [(h, m) for h in xs + ys + [other]]:
+    for peer in [(g, z) for z in zs] + [(h, m) for h in xs + ys + [other]]:
         pl.semaphore_signal(barrier, inc=1, device_id=peer, device_id_type=MESH)
-    pl.semaphore_wait(barrier, 9)
+    pl.semaphore_wait(barrier, 14)
 
     def remote(src, dst, send, recv, peer):
         return pltpu.make_async_remote_copy(
             src_ref=src, dst_ref=dst, send_sem=send, recv_sem=recv, device_id=peer, device_id_type=MESH
         )
 
-    def pass_on(slot):
-        peer = right if slot % 2 else left
-        return remote(
-            blocks.at[slot], blocks.at[slot + 2], bsend.at[slot + 2], brecv.at[slot + 2], (g, peer)
+    hops = []
+    for i, z in enumerate(zs):
+        hops.append(
+            (
+                remote(pay, blocks.at[i + 1], bsend.at[i], brecv.at[i], (g, z)),
+                remote(aux, sides.at[i + 1], ssend.at[i], srecv.at[i], (g, z)),
+            )
         )
-
-    hops = {
-        1: remote(pay, blocks.at[1], bsend.at[1], brecv.at[1], (g, right)),
-        2: remote(pay, blocks.at[2], bsend.at[2], brecv.at[2], (g, left)),
-    }
-    for slot in (1, 2, 3, 4, 5):
-        hops[slot + 2] = pass_on(slot)
-    hops[1].start()
-    hops[2].start()
-    base = pltpu.make_async_copy(pay, blocks.at[0], qloc.at[1])
-    base.start()
+    base = (
+        pltpu.make_async_copy(pay, blocks.at[0], qloc.at[1]),
+        pltpu.make_async_copy(aux, sides.at[0], qloc.at[2]),
+    )
+    for codes, side in [base] + hops:
+        side.start()
+        codes.start()
 
     half = NQ // 2
     top, bottom = pl.ds(0, half), pl.ds(half, half)
     near = [
-        remote(qrows.at[top], queries.at[py, px, core, top], psend.at[i], precv.at[i], (xs[i], m))
+        remote(qrows.at[top], queries.at[core, py, px, top], psend.at[i], precv.at[i], (xs[i], m))
         for i in range(3)
     ] + [
         remote(
-            qrows.at[bottom], queries.at[py, px, core, bottom], psend.at[3 + i], precv.at[3 + i], (ys[i], m)
+            qrows.at[bottom], queries.at[core, py, px, bottom], psend.at[3 + i], precv.at[3 + i], (ys[i], m)
         )
         for i in range(3)
     ]
-    row, column = queries.at[py, :, core, top], queries.at[:, px, core, bottom]
+    row, column = queries.at[core, py, :, top], queries.at[core, :, px, bottom]
     far = [remote(row, row, lsend.at[i], lrecv.at[i], (ys[i], m)) for i in range(3)] + [
         remote(column, column, lsend.at[3 + i], lrecv.at[3 + i], (xs[i], m)) for i in range(3)
     ]
-    mine = queries.at[:, :, core]
+    mine = queries.at[core]
     across = remote(mine, mine, csend.at[0], crecv.at[0], (other, m))
-    own = pltpu.make_async_copy(qrows, queries.at[py, px, core], qloc.at[0])
+    own = pltpu.make_async_copy(qrows, queries.at[core, py, px], qloc.at[0])
     for copy in near:
         copy.start()
     own.start()
@@ -276,68 +272,81 @@
     for ref in factor:
         ref[...] = jnp.zeros_like(ref)
 
-    base.wait()
-    eliminate(blocks[0], 192, True, *factor)
-    hops[1].wait_recv()
-    hops[2].wait_recv()
-    hops[3].start()
-    hops[4].start()
+    def step(slots, at):
+        for slot in slots:
+            if slot == 0:
+                base[0].wait()
+                base[1].wait()
+            else:
+                hops[slot - 1][0].wait_recv()
+                hops[slot - 1][1].wait_recv()
+        lo, hi = slots[0], slots[-1] + 1
+        eliminate(
+            blocks[lo:hi].reshape((hi - lo) * HIT, F), [sides[i] for i in slots], at, lo == 0, *factor
+        )
+
+    step((0,), 192)
     own.wait()
     for copy in near:
         copy.wait_recv()
     for copy in far:
         copy.start()
-    eliminate(blocks[1:3].reshape(2 * HIT, PAY), 0, False, *factor)
-    hops[3].wait_recv()
-    hops[4].wait_recv()
-    hops[5].start()
-    hops[6].start()
-    eliminate(blocks[3:5].reshape(2 * HIT, PAY), 64, False, *factor)
-    hops[5].wait_recv()
-    hops[6].wait_recv()
-    hops[7].start()
-    eliminate(blocks[5:7].reshape(2 * HIT, PAY), 128, False, *factor)
+    step((1, 2), 0)
+    step((3, 4), 64)
+    step((5, 6), 128)
     for copy in far:
         copy.wait_recv()
     across.start()
-    hops[7].wait_recv()
-    eliminate(blocks[7], 224, False, *factor)
+    step((7,), 224)
+
+    def half_lines(which):
+        return evaluate(queries.at[which].reshape(16, NQ, F), tt_hi, tt_lo, tt_row)
+
+    near_half = half_lines(core)
     across.wait_recv()
-    evaluate(queries.reshape(16, 2, NQ, F), tt_hi, tt_lo, tt_row, out)
-
-    for slot in range(1, 8):
-        hops[slot].wait_send()
+    far_half = half_lines(1 - core)
+    for i in range(2):
+        even = jnp.where(core == 0, near_half[i], far_half[i])
+        odd = jnp.where(core == 0, far_half[i], near_half[i])
+        for side in range(2):
+            lanes = slice(NQ * side, NQ * (side + 1))
+            out[i, :, side, :] = jnp.concatenate([even[:, lanes], odd[:, lanes]], axis=1)
+
+    for codes, side in hops:
+        codes.wait_send()
+        side.wait_send()
     for copy in near + far + [across]:
         copy.wait_send()
 
 
-def group_posterior(n_mem, pay, qrows):
+def group_posterior(n_mem, pay, aux, qrows):
     vmem = pl.BlockSpec(memory_space=pltpu.VMEM)
     dma = pltpu.SemaphoreType.DMA
     return pl.pallas_call(
         functools.partial(group_kernel, n_mem),
-        out_shape=jax.ShapeDtypeStruct((2, 4, 4, 128), F32),
-        in_specs=[pl.BlockSpec(memory_space=pl.ANY)] * 2,
+        out_shape=jax.ShapeDtypeStruct((2, 8, 2, 128), F32),
+        in_specs=[pl.BlockSpec(memory_space=pl.ANY)] * 3,
         out_specs=vmem,
         scratch_shapes=[
-            pltpu.VMEM((n_mem, HIT, PAY), BF16),
-            pltpu.VMEM((4, 4, 2, NQ, F), BF16),
+            pltpu.VMEM((n_mem, HIT, F), jnp.int16),
+            pltpu.VMEM((n_mem, 8, 128), F32),
+            pltpu.VMEM((2, 4, 4, NQ, F), BF16),
             pltpu.VMEM((256, FU), BF16),
             pltpu.VMEM((256, FU), BF16),
             pltpu.VMEM((FU, 256), BF16),
             pltpu.VMEM((FU, 256), BF16),
             pltpu.VMEM((8, 256), F32),
-            dma((8,)), dma((8,)), dma((2,)), dma((6,)), dma((6,)), dma((6,)), dma((6,)), dma((1,)), dma((1,)),
+            dma((7,)), dma((7,)), dma((7,)), dma((7,)), dma((3,)), dma((6,)), dma((6,)), dma((6,)), dma((6,)), dma((1,)), dma((1,)),
         ],
         compiler_params=pltpu.CompilerParams(
-            collective_id=0, has_side_effects=True, vmem_limit_bytes=48 << 20
+            collective_id=0, has_side_effects=True, vmem_limit_bytes=63 << 20
         ),
         name="group_posterior",
-    )(pay, qrows)
+    )(pay, aux, qrows)
 
 
 def on_device(n_mem, voxels, conv_weight, conv_bias, row_counts, sample_patch, targets, query_patch):
-    pay, qrows = features(
+    pay, aux, qrows = features(
         voxels.transpose(1, 2, 0, 3),
         conv_weight,
         conv_bias.reshape(1, C),
@@ -346,7 +355,7 @@
         targets.reshape(1, -1),
         query_patch.reshape(1, -1),
     )
-    out = group_posterior(n_mem, pay, qrows)
+    out = group_posterior(n_mem, pay, aux, qrows)
     return out[0].reshape(1, 1, -1), out[1].reshape(1, 1, -1)
 
 

time: 40.6 us -> 39 us (0.961)
  local copies, waits for them, and re-layouts: 2.32 us -> 1.32 us
  Pallas kernels: 36.7 us -> 36.1 us
    unnamed x4 -> x0, local copies, waits for them, and re-layouts: 1.72 us -> none
    slice x1, local copies, waits for them, and re-layouts: 0.61 us -> 1.32 us  [on_device(): return (out[0].reshape(1, 1, -1), out[1].reshape(1, 1, -1))]
    pallas_call x1, Pallas kernels: 28.9 us -> 28.3 us  [group_posterior(): pl.pallas_call(functools.partial(group_kernel, n_mem), out_shape=jax.Shap...]
where the time goes in v3:
time: 39 us; the launch traced here: 38.7 us
  Pallas kernels  36.1 us (93%)
  local copies, waits for them, and re-layouts  1.32 us (3%)
  between operations  1.29 us (3%)
    pallas_call x1, Pallas kernels, group_posterior(): pl.pallas_call(functools.partial(group_kernel, n_mem), out_shape=jax.Shap...  28.3 us
    pallas_call x1, Pallas kernels, features(): pl.pallas_call(feature_kernel, out_shape=(jax.ShapeDtypeStruct((HIT, F),...  7.84 us
    slice x1, local copies, waits for them, and re-layouts, on_device(): return (out[0].reshape(1, 1, -1), out[1].reshape(1, 1, -1))  1.32 us

profile of v3, /device:TPU:1, one launch (start us, length us, event | category | flops | bytes accessed | tf_op | source)
XLA Modules:
  0.0 38.7 jit_solution(7241145421218679441)
XLA Ops:
  1.3 7.8 %features.1 = (s16[32,512]{1,0:T(8,128)(2,1)}, f32[8,128]{1,0:T(8,128)}, bf16[64,512]{1,0:T(8,128)(2,1)}) custom-call(s32[1]{0:T(128)S(6)} %copy.9.count, bf16[6,6,128,384]{3,2,1,0:T(8,128)(2,1)} %bitcast.7, bf16[3,3,3,64,64]{4,3,2,1,0:T(8,128)(2,1)} %weight.1, f32[1,64]{1,0:T(1,128)} %bitcast.12, s32[1,2048]{1,0:T(1,128)} %bitcast.8, f32[1,2048]{1,0:T(1,128)} %bitcast.9, ...), custom_call_target="tpu_custom_call" | custom-call | tf_op jit(solution)/shard_map/features/pallas_call | solution.py:104
  9.1 28.3 %group_posterior.1 = f32[2,8,2,128]{3,2,1,0:T(2,128)} custom-call(s16[32,512]{1,0:T(8,128)(2,1)} %get-tuple-element.5.pay, f32[8,128]{1,0:T(8,128)} %get-tuple-element.6.aux, bf16[64,512]{1,0:T(8,128)(2,1)} %get-tuple-element.7.qrows), custom_call_target="tpu_custom_call" | custom-call | tf_op jit(solution)/shard_map/group_posterior/pallas_call | solution.py:325
  37.4 1.3 %fusion = (f32[1,8,2,128]{3,2,1,0:T(2,128)}, f32[1,8,2,128]{3,2,1,0:T(2,128)}) fusion(f32[2,8,2,128]{3,2,1,0:T(2,128)} %group_posterior.1), kind=kLoop, calls=%fused_computation | loop fusion | bytes 32768 | tf_op jit(solution)/shard_map/slice | solution.py:359

commit v4 on v3

--- a/solution.py
+++ b/solution.py
@@ -48,7 +48,7 @@
                 band[row : row + C, 2 * C :] = jnp.concatenate([at(zi - 1), at(zi - 3)], axis=1)
 
 
-def feature_kernel(
+def features(
     count, vox, weight, bias, ids, targets, qids, pay, aux, qrows, slab, taps, band, feats, sem, wsem
 ):
     copies = [pltpu.make_async_copy(vox.at[x], slab.at[x], sem.at[x]) for x in range(EDGE)]
@@ -93,34 +93,9 @@
     pay[...] = jnp.round(rows * unit).astype(jnp.int32).astype(jnp.int16)
     lane = iota((HIT, 128), 1)
     sides = jnp.where(lane == 0, scaled, jnp.where(lane == 1, peak * (root * (1.0 / TOP)), 0.0))
-    aux[...] = jnp.zeros_like(aux)
-    aux[:, :HIT] = sides.T[:8, :]
+    aux[...] = jnp.concatenate([sides.T[:8, :], jnp.zeros((8, 128 - HIT), F32)], axis=1)
     pick = (iota((NP, NQ), 0) == qids[...]).astype(F32).astype(BF16)
     qrows[...] = dot(pick, feats[...].astype(BF16), 0, 0).astype(BF16)
-
-
-def features(vox, weight, bias, count, ids, targets, qids):
-    vmem, hbm = pl.BlockSpec(memory_space=pltpu.VMEM), pl.BlockSpec(memory_space=pl.ANY)
-    return pl.pallas_call(
-        feature_kernel,
-        out_shape=(
-            jax.ShapeDtypeStruct((HIT, F), jnp.int16),
-            jax.ShapeDtypeStruct((8, 128), F32),
-            jax.ShapeDtypeStruct((NQ, F), BF16),
-        ),
-        in_specs=[pl.BlockSpec(memory_space=pltpu.SMEM), hbm, hbm, vmem, vmem, vmem, vmem],
-        out_specs=(vmem, vmem, vmem),
-        scratch_shapes=[
-            pltpu.VMEM((EDGE, EDGE, NP, EDGE * C), BF16),
-            pltpu.VMEM((3, 3, 3, C, C), BF16),
-            pltpu.VMEM((9 * EDGE * C, 4 * C), BF16),
-            pltpu.VMEM((NP, F), F32),
-            pltpu.SemaphoreType.DMA((EDGE,)),
-            pltpu.SemaphoreType.DMA((1,)),
-        ],
-        compiler_params=pltpu.CompilerParams(vmem_limit_bytes=56 << 20),
-        name="features",
-    )(count, vox, weight, bias, ids, targets, qids)
 
 
 def spread(x, shape=(8, 128)):
@@ -208,9 +183,9 @@
 
 
 def group_kernel(
-    n_mem, pay, aux, qrows, out,
-    blocks, sides, queries, t_hi, t_lo, tt_hi, tt_lo, tt_row,
-    bsend, brecv, ssend, srecv, qloc, psend, precv, lsend, lrecv, csend, crecv,
+    n_mem, count, vox, weight, bias, ids, targets, qids, out,
+    slab, taps, band, feats, blocks, sides, queries, t_hi, t_lo, tt_hi, tt_lo, tt_row,
+    sem, wsem, bsend, brecv, ssend, srecv, psend, precv, lsend, lrecv, csend, crecv,
 ):
     g, m = lax.axis_index("grp"), lax.axis_index("mem")
     core, plane = lax.rem(g, 2), lax.div(g, 2)
@@ -223,6 +198,14 @@
     barrier = pltpu.get_barrier_semaphore()
     for peer in [(g, z) for z in zs] + [(h, m) for h in xs + ys + [other]]:
         pl.semaphore_signal(barrier, inc=1, device_id=peer, device_id_type=MESH)
+
+    factor = (t_hi, t_lo, tt_hi, tt_lo, tt_row)
+    for ref in factor:
+        ref[...] = jnp.zeros_like(ref)
+    pay, aux, qrows = blocks.at[0], sides.at[0], queries.at[core, py, px]
+    features(
+        count, vox, weight, bias, ids, targets, qids, pay, aux, qrows, slab, taps, band, feats, sem, wsem
+    )
     pl.semaphore_wait(barrier, 14)
 
     def remote(src, dst, send, recv, peer):
@@ -238,11 +221,7 @@
                 remote(aux, sides.at[i + 1], ssend.at[i], srecv.at[i], (g, z)),
             )
         )
-    base = (
-        pltpu.make_async_copy(pay, blocks.at[0], qloc.at[1]),
-        pltpu.make_async_copy(aux, sides.at[0], qloc.at[2]),
-    )
-    for codes, side in [base] + hops:
+    for codes, side in hops:
         side.start()
         codes.start()
 
@@ -261,23 +240,17 @@
     far = [remote(row, row, lsend.at[i], lrecv.at[i], (ys[i], m)) for i in range(3)] + [
         remote(column, column, lsend.at[3 + i], lrecv.at[3 + i], (xs[i], m)) for i in range(3)
     ]
-    mine = queries.at[core]
-    across = remote(mine, mine, csend.at[0], crecv.at[0], (other, m))
-    own = pltpu.make_async_copy(qrows, queries.at[core, py, px], qloc.at[0])
+    pieces = []
+    for i, shift in enumerate((0, 1, 2, 3)):
+        wy, wx = lax.rem(py + 4 - shift, 4), lax.rem(px + 4 - shift, 4)
+        for j, piece in enumerate((queries.at[core, wy, :, top], queries.at[core, :, wx, bottom])):
+            pieces.append(remote(piece, piece, csend.at[2 * i + j], crecv.at[2 * i + j], (other, m)))
     for copy in near:
         copy.start()
-    own.start()
-
-    factor = (t_hi, t_lo, tt_hi, tt_lo, tt_row)
-    for ref in factor:
-        ref[...] = jnp.zeros_like(ref)
 
     def step(slots, at):
         for slot in slots:
-            if slot == 0:
-                base[0].wait()
-                base[1].wait()
-            else:
+            if slot > 0:
                 hops[slot - 1][0].wait_recv()
                 hops[slot - 1][1].wait_recv()
         lo, hi = slots[0], slots[-1] + 1
@@ -286,48 +259,58 @@
         )
 
     step((0,), 192)
-    own.wait()
     for copy in near:
         copy.wait_recv()
-    for copy in far:
+    for i in (0, 3, 2, 5, 1, 4):
+        far[i].start()
+    for copy in pieces[:2]:
         copy.start()
     step((1, 2), 0)
     step((3, 4), 64)
+    for i in (0, 2):
+        for j in range(2):
+            far[3 * j + i].wait_recv()
+            pieces[2 * (i + 1) + j].start()
     step((5, 6), 128)
-    for copy in far:
-        copy.wait_recv()
-    across.start()
+    for j in range(2):
+        far[3 * j + 1].wait_recv()
+        pieces[4 + j].start()
     step((7,), 224)
 
     def half_lines(which):
         return evaluate(queries.at[which].reshape(16, NQ, F), tt_hi, tt_lo, tt_row)
 
     near_half = half_lines(core)
-    across.wait_recv()
+    for copy in pieces:
+        copy.wait_recv()
     far_half = half_lines(1 - core)
     for i in range(2):
         even = jnp.where(core == 0, near_half[i], far_half[i])
         odd = jnp.where(core == 0, far_half[i], near_half[i])
         for side in range(2):
             lanes = slice(NQ * side, NQ * (side + 1))
-            out[i, :, side, :] = jnp.concatenate([even[:, lanes], odd[:, lanes]], axis=1)
+            out[i, pl.ds(side, 8, stride=2), :] = jnp.concatenate([even[:, lanes], odd[:, lanes]], axis=1)
 
     for codes, side in hops:
         codes.wait_send()
         side.wait_send()
-    for copy in near + far + [across]:
+    for copy in near + far + pieces:
         copy.wait_send()
 
 
-def group_posterior(n_mem, pay, aux, qrows):
-    vmem = pl.BlockSpec(memory_space=pltpu.VMEM)
+def group_posterior(n_mem, count, vox, weight, bias, ids, targets, qids):
+    vmem, hbm = pl.BlockSpec(memory_space=pltpu.VMEM), pl.BlockSpec(memory_space=pl.ANY)
     dma = pltpu.SemaphoreType.DMA
     return pl.pallas_call(
         functools.partial(group_kernel, n_mem),
-        out_shape=jax.ShapeDtypeStruct((2, 8, 2, 128), F32),
-        in_specs=[pl.BlockSpec(memory_space=pl.ANY)] * 3,
+        out_shape=jax.ShapeDtypeStruct((2, 16, 128), F32),
+        in_specs=[pl.BlockSpec(memory_space=pltpu.SMEM), hbm, hbm, vmem, vmem, vmem, vmem],
         out_specs=vmem,
         scratch_shapes=[
+            pltpu.VMEM((EDGE, EDGE, NP, EDGE * C), BF16),
+            pltpu.VMEM((3, 3, 3, C, C), BF16),
+            pltpu.VMEM((9 * EDGE * C, 4 * C), BF16),
+            pltpu.VMEM((NP, F), F32),
             pltpu.VMEM((n_mem, HIT, F), jnp.int16),
             pltpu.VMEM((n_mem, 8, 128), F32),
             pltpu.VMEM((2, 4, 4, NQ, F), BF16),
@@ -336,26 +319,27 @@
             pltpu.VMEM((FU, 256), BF16),
             pltpu.VMEM((FU, 256), BF16),
             pltpu.VMEM((8, 256), F32),
-            dma((7,)), dma((7,)), dma((7,)), dma((7,)), dma((3,)), dma((6,)), dma((6,)), dma((6,)), dma((6,)), dma((1,)), dma((1,)),
+            dma((EDGE,)), dma((1,)), dma((7,)), dma((7,)), dma((7,)), dma((7,)),
+            dma((6,)), dma((6,)), dma((6,)), dma((6,)), dma((8,)), dma((8,)),
         ],
         compiler_params=pltpu.CompilerParams(
             collective_id=0, has_side_effects=True, vmem_limit_bytes=63 << 20
         ),
         name="group_posterior",
-    )(pay, aux, qrows)
+    )(count, vox, weight, bias, ids, targets, qids)
 
 
 def on_device(n_mem, voxels, conv_weight, conv_bias, row_counts, sample_patch, targets, query_patch):
-    pay, aux, qrows = features(
+    out = group_posterior(
+        n_mem,
+        row_counts,
         voxels.transpose(1, 2, 0, 3),
         conv_weight,
         conv_bias.reshape(1, C),
-        row_counts,
         sample_patch.reshape(1, -1),
         targets.reshape(1, -1),
         query_patch.reshape(1, -1),
     )
-    out = group_posterior(n_mem, pay, aux, qrows)
     return out[0].reshape(1, 1, -1), out[1].reshape(1, 1, -1)
 
 

time: 39 us -> 34.2 us (0.88)
  the two profiles are of different devices: /device:TPU:1 before, /device:TPU:14 now
where the time goes in v4:
time: 34.2 us; the launch traced here: 34 us
  Pallas kernels  31.4 us (92%)
  local copies, waits for them, and re-layouts  1.32 us (4%)
  between operations  1.29 us (4%)
    pallas_call x1, Pallas kernels, group_posterior(): pl.pallas_call(functools.partial(group_kernel, n_mem), out_shape=jax.Shap...  31.4 us
    slice x1, local copies, waits for them, and re-layouts, on_device(): return (out[0].reshape(1, 1, -1), out[1].reshape(1, 1, -1))  1.32 us

profile of v4, /device:TPU:14, one launch (start us, length us, event | category | flops | bytes accessed | tf_op | source)
XLA Modules:
  0.0 34.0 jit_solution(8232651559598418213)
XLA Ops:
  1.3 31.4 %group_posterior.1 = f32[2,16,128]{2,1,0:T(8,128)} custom-call(s32[1]{0:T(128)S(6)} %copy.9.count, bf16[6,6,128,384]{3,2,1,0:T(8,128)(2,1)} %bitcast.7, bf16[3,3,3,64,64]{4,3,2,1,0:T(8,128)(2,1)} %weight.1, f32[1,64]{1,0:T(1,128)} %bitcast.12, s32[1,2048]{1,0:T(1,128)} %bitcast.8, f32[1,2048]{1,0:T(1,128)} %bitcast.9, s32[1,64]{1,0:T(1,128)} %bitcast.13), custom_call_target="tpu_custom_call" | custom-call | tf_op jit(solution)/shard_map/group_posterior/pallas_call | solution.py:304
  32.7 1.3 %fusion = (f32[1,16,128]{2,1,0:T(8,128)}, f32[1,16,128]{2,1,0:T(8,128)}) fusion(f32[2,16,128]{2,1,0:T(8,128)} %group_posterior.1), kind=kLoop, calls=%fused_computation | loop fusion | bytes 32768 | tf_op jit(solution)/shard_map/slice | solution.py:343

commit v5 on v4

--- a/solution.py
+++ b/solution.py
@@ -48,54 +48,40 @@
                 band[row : row + C, 2 * C :] = jnp.concatenate([at(zi - 1), at(zi - 3)], axis=1)
 
 
-def features(
-    count, vox, weight, bias, ids, targets, qids, pay, aux, qrows, slab, taps, band, feats, sem, wsem
-):
-    copies = [pltpu.make_async_copy(vox.at[x], slab.at[x], sem.at[x]) for x in range(EDGE)]
-    taps_in = pltpu.make_async_copy(weight, taps, wsem.at[0])
-    taps_in.start()
-    for copy in copies:
-        copy.start()
-
+def patch_features(slab, band, shift, part, feats):
+    own = slice(HIT * part, HIT * (part + 1))
+    lhs = jnp.concatenate(
+        [
+            slab[dx : dx + 4, dy : dy + 4, own].reshape(16 * HIT, EDGE * C)
+            for dx in range(3)
+            for dy in range(3)
+        ],
+        axis=1,
+    )
+    act = jnp.tanh(dot(lhs, band[...]) + shift).reshape(2, 2, 2, 2, HIT, 4 * C)
+    for cx in range(2):
+        for cy in range(2):
+            cell = (act[cx, 0, cy, 0] + act[cx, 0, cy, 1]) + (act[cx, 1, cy, 0] + act[cx, 1, cy, 1])
+            at = (2 * cx + cy) * 2 * C
+            feats[own, at : at + 2 * C] = (cell[:, : 2 * C] + cell[:, 2 * C :]) * 0.125
+
+
+def hit_sums(count, ids, targets):
     live = iota((HIT, ids.shape[1]), 1) < count[0]
     mine = jnp.logical_and(ids[...] == iota((HIT, ids.shape[1]), 0), live)
     hits = jnp.sum(jnp.where(mine, 1.0, 0.0), axis=1, keepdims=True)
     tsum = jnp.sum(jnp.where(mine, targets[...], 0.0), axis=1, keepdims=True)
     root = jnp.sqrt(hits)
-    scaled = jnp.where(hits > 0, tsum / jnp.where(hits > 0, root, 1.0), 0.0)
-    taps_in.wait()
-    fill_band(taps, band)
-    shift = jnp.concatenate([bias[...]] * 4, axis=1)
-    waited = 0
-    for cx in range(2):
-        while waited < 2 * cx + 4:
-            copies[waited].wait()
-            waited += 1
-        for cy in range(2):
-            lhs = jnp.concatenate(
-                [
-                    slab[2 * cx + dx : 2 * cx + dx + 2, 2 * cy + dy : 2 * cy + dy + 2].reshape(
-                        4 * NP, EDGE * C
-                    )
-                    for dx in range(3)
-                    for dy in range(3)
-                ],
-                axis=1,
-            )
-            act = jnp.tanh(dot(lhs, band[...]) + shift).reshape(4, NP, 4 * C)
-            pooled = (act[0] + act[1]) + (act[2] + act[3])
-            cell = (pooled[:, : 2 * C] + pooled[:, 2 * C :]) * 0.125
-            feats[:, (2 * cx + cy) * 2 * C : (2 * cx + cy + 1) * 2 * C] = cell
-
-    rows = feats[:HIT, :]
+    return root, jnp.where(hits > 0, tsum / jnp.where(hits > 0, root, 1.0), 0.0)
+
+
+def code_rows(rows, root, scaled, pay, aux):
     peak = jnp.max(jnp.abs(rows), axis=1, keepdims=True)
     unit = jnp.where(peak > 0, TOP / jnp.where(peak > 0, peak, 1.0), 0.0)
     pay[...] = jnp.round(rows * unit).astype(jnp.int32).astype(jnp.int16)
     lane = iota((HIT, 128), 1)
     sides = jnp.where(lane == 0, scaled, jnp.where(lane == 1, peak * (root * (1.0 / TOP)), 0.0))
     aux[...] = jnp.concatenate([sides.T[:8, :], jnp.zeros((8, 128 - HIT), F32)], axis=1)
-    pick = (iota((NP, NQ), 0) == qids[...]).astype(F32).astype(BF16)
-    qrows[...] = dot(pick, feats[...].astype(BF16), 0, 0).astype(BF16)
 
 
 def spread(x, shape=(8, 128)):
@@ -110,25 +96,41 @@
     sub = iota((8, 128), 0)
     count = n // 8
     rows = [wide[8 * b : 8 * b + 8] for b in range(count)]
+
+    def columns(t, b):
+        return [spread(rows[t][:, 8 * b + c : 8 * b + c + 1]) for c in range(8)]
+
     done = []
+    diagonal = columns(0, 0)
     for b in range(count):
-        cols = [
-            [spread(rows[t][:, 8 * b + c : 8 * b + c + 1]) for c in range(8)] for t in range(b, count)
-        ]
+        cols = {t: columns(t, b) for t in range(b + 1, count)}
+        cols[b] = diagonal
+        ahead = b + 1 < count
+        if ahead:
+            coming, taken = columns(b + 1, b + 1), [None] * 8
         for j in range(8):
-            heads = [spread(cols[0][c][j : j + 1, :]) for c in range(j, 8)]
+            heads = [spread(cols[b][c][j : j + 1, :]) for c in range(j, 8)]
             inv = 1.0 / heads[0]
-            row = spread(rows[b][j : j + 1, :]) * inv
-            heads = [h * inv for h in heads]
-            for t in range(count - b):
-                below = jnp.where(sub > j, cols[0][j], 0.0) if t == 0 else cols[t][j]
-                rows[b + t] = rows[b + t] - below * row
+            times = {
+                t: (jnp.where(sub > j, cols[t][j], 0.0) if t == b else cols[t][j]) * inv
+                for t in range(b, count)
+            }
+            row = spread(rows[b][j : j + 1, :])
+            for t in range(b, count):
                 for c in range(j + 1, 8):
-                    cols[t][c] = cols[t][c] - below * heads[c - j]
-        diag = cols[0][0]
+                    cols[t][c] = cols[t][c] - times[t] * heads[c - j]
+            for t in range(b, count):
+                rows[t] = rows[t] - times[t] * row
+            if ahead:
+                for c in range(8):
+                    term = times[b + 1] * spread(cols[b + 1][j][c : c + 1, :])
+                    taken[c] = term if taken[c] is None else taken[c] + term
+        pivots = cols[b][0]
         for j in range(1, 8):
-            diag = jnp.where(sub == j, cols[0][j], diag)
-        done.append(rows[b] * lax.rsqrt(diag))
+            pivots = jnp.where(sub == j, cols[b][j], pivots)
+        done.append(rows[b] * lax.rsqrt(pivots))
+        if ahead:
+            diagonal = [coming[c] - taken[c] for c in range(8)]
     return jnp.concatenate(done, axis=0)[:, n : 2 * n]
 
 
@@ -183,8 +185,8 @@
 
 
 def group_kernel(
-    n_mem, count, vox, weight, bias, ids, targets, qids, out,
-    slab, taps, band, feats, blocks, sides, queries, t_hi, t_lo, tt_hi, tt_lo, tt_row,
+    n_mem, count, vox, weight, bias_in, ids_in, targets_in, qids_in, out,
+    bias, ids, targets, qids, slab, taps, band, feats, blocks, sides, queries, t_hi, t_lo, tt_hi, tt_lo, tt_row,
     sem, wsem, bsend, brecv, ssend, srecv, psend, precv, lsend, lrecv, csend, crecv,
 ):
     g, m = lax.axis_index("grp"), lax.axis_index("mem")
@@ -199,13 +201,35 @@
     for peer in [(g, z) for z in zs] + [(h, m) for h in xs + ys + [other]]:
         pl.semaphore_signal(barrier, inc=1, device_id=peer, device_id_type=MESH)
 
+    taps_in = pltpu.make_async_copy(weight, taps, wsem.at[0])
+    small = [
+        pltpu.make_async_copy(src, dst, wsem.at[i + 1])
+        for i, (src, dst) in enumerate(
+            ((bias_in, bias), (ids_in, ids), (targets_in, targets), (qids_in, qids))
+        )
+    ]
+    for copy in [taps_in] + small:
+        copy.start()
+    parts = []
+    for p in range(NP // HIT):
+        own = pl.ds(HIT * p, HIT)
+        parts.append(pltpu.make_async_copy(vox.at[:, :, own], slab.at[:, :, own], sem.at[p]))
+        parts[p].start()
+
     factor = (t_hi, t_lo, tt_hi, tt_lo, tt_row)
     for ref in factor:
         ref[...] = jnp.zeros_like(ref)
+    for copy in small:
+        copy.wait()
+    root, scaled = hit_sums(count, ids, targets)
+    shift = jnp.concatenate([bias[...]] * 4, axis=1)
+    taps_in.wait()
+    fill_band(taps, band)
     pay, aux, qrows = blocks.at[0], sides.at[0], queries.at[core, py, px]
-    features(
-        count, vox, weight, bias, ids, targets, qids, pay, aux, qrows, slab, taps, band, feats, sem, wsem
-    )
+
+    parts[0].wait()
+    patch_features(slab, band, shift, 0, feats)
+    code_rows(feats[:HIT, :], root, scaled, pay, aux)
     pl.semaphore_wait(barrier, 14)
 
     def remote(src, dst, send, recv, peer):
@@ -224,6 +248,12 @@
     for codes, side in hops:
         side.start()
         codes.start()
+
+    for p in range(1, NP // HIT):
+        parts[p].wait()
+        patch_features(slab, band, shift, p, feats)
+    pick = (iota((NP, NQ), 0) == qids[...]).astype(F32).astype(BF16)
+    qrows[...] = dot(pick, feats[...].astype(BF16), 0, 0).astype(BF16)
 
     half = NQ // 2
     top, bottom = pl.ds(0, half), pl.ds(half, half)
@@ -259,23 +289,23 @@
         )
 
     step((0,), 192)
+    step((1, 2), 0)
     for copy in near:
         copy.wait_recv()
     for i in (0, 3, 2, 5, 1, 4):
         far[i].start()
     for copy in pieces[:2]:
         copy.start()
-    step((1, 2), 0)
     step((3, 4), 64)
+    step((5, 6), 128)
     for i in (0, 2):
         for j in range(2):
             far[3 * j + i].wait_recv()
             pieces[2 * (i + 1) + j].start()
-    step((5, 6), 128)
+    step((7,), 224)
     for j in range(2):
         far[3 * j + 1].wait_recv()
         pieces[4 + j].start()
-    step((7,), 224)
 
     def half_lines(which):
         return evaluate(queries.at[which].reshape(16, NQ, F), tt_hi, tt_lo, tt_row)
@@ -299,14 +329,18 @@
 
 
 def group_posterior(n_mem, count, vox, weight, bias, ids, targets, qids):
-    vmem, hbm = pl.BlockSpec(memory_space=pltpu.VMEM), pl.BlockSpec(memory_space=pl.ANY)
+    vmem, hbm = pl.BlockSpec(memory_space=pltpu.VMEM), pl.BlockSpec(memory_space=pltpu.HBM)
     dma = pltpu.SemaphoreType.DMA
     return pl.pallas_call(
         functools.partial(group_kernel, n_mem),
         out_shape=jax.ShapeDtypeStruct((2, 16, 128), F32),
-        in_specs=[pl.BlockSpec(memory_space=pltpu.SMEM), hbm, hbm, vmem, vmem, vmem, vmem],
+        in_specs=[pl.BlockSpec(memory_space=pltpu.SMEM), hbm, hbm, hbm, hbm, hbm, hbm],
         out_specs=vmem,
         scratch_shapes=[
+            pltpu.VMEM((1, C), F32),
+            pltpu.VMEM(ids.shape, jnp.int32),
+            pltpu.VMEM(ids.shape, F32),
+            pltpu.VMEM((1, NQ), jnp.int32),
             pltpu.VMEM((EDGE, EDGE, NP, EDGE * C), BF16),
             pltpu.VMEM((3, 3, 3, C, C), BF16),
             pltpu.VMEM((9 * EDGE * C, 4 * C), BF16),
@@ -319,11 +353,11 @@
             pltpu.VMEM((FU, 256), BF16),
             pltpu.VMEM((FU, 256), BF16),
             pltpu.VMEM((8, 256), F32),
-            dma((EDGE,)), dma((1,)), dma((7,)), dma((7,)), dma((7,)), dma((7,)),
+            dma((NP // HIT,)), dma((5,)), dma((7,)), dma((7,)), dma((7,)), dma((7,)),
             dma((6,)), dma((6,)), dma((6,)), dma((6,)), dma((8,)), dma((8,)),
         ],
         compiler_params=pltpu.CompilerParams(
-            collective_id=0, has_side_effects=True, vmem_limit_bytes=63 << 20
+            collective_id=0, has_side_effects=True, vmem_limit_bytes=61 << 20
         ),
         name="group_posterior",
     )(count, vox, weight, bias, ids, targets, qids)

time: 34.2 us -> 35.7 us (1.044)
  the two profiles are of different devices: /device:TPU:14 before, /device:TPU:1 now
where the time goes in v5:
time: 35.7 us; the launch traced here: 35.6 us
  Pallas kernels  33 us (92%)
  local copies, waits for them, and re-layouts  1.32 us (4%)
  between operations  1.29 us (4%)
    pallas_call x1, Pallas kernels, group_posterior(): pl.pallas_call(functools.partial(group_kernel, n_mem), out_shape=jax.Shap...  33 us
    slice x1, local copies, waits for them, and re-layouts, on_device(): return (out[0].reshape(1, 1, -1), out[1].reshape(1, 1, -1))  1.32 us

profile of v5, /device:TPU:1, one launch (start us, length us, event | category | flops | bytes accessed | tf_op | source)
XLA Modules:
  0.0 35.6 jit_solution(6636988931050088532)
XLA Ops:
  1.3 33.0 %group_posterior.1 = f32[2,16,128]{2,1,0:T(8,128)} custom-call(s32[1]{0:T(128)S(6)} %copy.9.count, bf16[6,6,128,384]{3,2,1,0:T(8,128)(2,1)} %bitcast.7, bf16[3,3,3,64,64]{4,3,2,1,0:T(8,128)(2,1)} %weight.1, f32[1,64]{1,0:T(1,128)} %bitcast.12, s32[1,2048]{1,0:T(1,128)} %bitcast.8, f32[1,2048]{1,0:T(1,128)} %bitcast.9, s32[1,64]{1,0:T(1,128)} %bitcast.13), custom_call_target="tpu_custom_call" | custom-call | tf_op jit(solution)/shard_map/group_posterior/pallas_call | solution.py:334
  34.3 1.3 %fusion = (f32[1,16,128]{2,1,0:T(8,128)}, f32[1,16,128]{2,1,0:T(8,128)}) fusion(f32[2,16,128]{2,1,0:T(8,128)} %group_posterior.1), kind=kLoop, calls=%fused_computation | loop fusion | bytes 32768 | tf_op jit(solution)/shard_map/slice | solution.py:377

commit v6 on v4

--- a/solution.py
+++ b/solution.py
@@ -110,25 +110,41 @@
     sub = iota((8, 128), 0)
     count = n // 8
     rows = [wide[8 * b : 8 * b + 8] for b in range(count)]
+
+    def columns(t, b):
+        return [spread(rows[t][:, 8 * b + c : 8 * b + c + 1]) for c in range(8)]
+
     done = []
+    diagonal = columns(0, 0)
     for b in range(count):
-        cols = [
-            [spread(rows[t][:, 8 * b + c : 8 * b + c + 1]) for c in range(8)] for t in range(b, count)
-        ]
+        cols = {t: columns(t, b) for t in range(b + 1, count)}
+        cols[b] = diagonal
+        ahead = b + 1 < count
+        if ahead:
+            coming, taken = columns(b + 1, b + 1), [None] * 8
         for j in range(8):
-            heads = [spread(cols[0][c][j : j + 1, :]) for c in range(j, 8)]
+            heads = [spread(cols[b][c][j : j + 1, :]) for c in range(j, 8)]
             inv = 1.0 / heads[0]
-            row = spread(rows[b][j : j + 1, :]) * inv
-            heads = [h * inv for h in heads]
-            for t in range(count - b):
-                below = jnp.where(sub > j, cols[0][j], 0.0) if t == 0 else cols[t][j]
-                rows[b + t] = rows[b + t] - below * row
+            times = {
+                t: (jnp.where(sub > j, cols[t][j], 0.0) if t == b else cols[t][j]) * inv
+                for t in range(b, count)
+            }
+            row = spread(rows[b][j : j + 1, :])
+            for t in range(b, count):
                 for c in range(j + 1, 8):
-                    cols[t][c] = cols[t][c] - below * heads[c - j]
-        diag = cols[0][0]
+                    cols[t][c] = cols[t][c] - times[t] * heads[c - j]
+            for t in range(b, count):
+                rows[t] = rows[t] - times[t] * row
+            if ahead:
+                for c in range(8):
+                    term = times[b + 1] * spread(cols[b + 1][j][c : c + 1, :])
+                    taken[c] = term if taken[c] is None else taken[c] + term
+        pivots = cols[b][0]
         for j in range(1, 8):
-            diag = jnp.where(sub == j, cols[0][j], diag)
-        done.append(rows[b] * lax.rsqrt(diag))
+            pivots = jnp.where(sub == j, cols[b][j], pivots)
+        done.append(rows[b] * lax.rsqrt(pivots))
+        if ahead:
+            diagonal = [coming[c] - taken[c] for c in range(8)]
     return jnp.concatenate(done, axis=0)[:, n : 2 * n]
 
 

time: 34.2 us -> 31.9 us (0.933)
  the two profiles are of different devices: /device:TPU:14 before, /device:TPU:1 now
where the time goes in v6:
time: 31.9 us; the launch traced here: 31.4 us
  Pallas kernels  28.8 us (90%)
  local copies, waits for them, and re-layouts  1.32 us (4%)
  between operations  1.29 us (4%)
    pallas_call x1, Pallas kernels, group_posterior(): pl.pallas_call(functools.partial(group_kernel, n_mem), out_shape=jax.Shap...  28.8 us
    slice x1, local copies, waits for them, and re-layouts, on_device(): return (out[0].reshape(1, 1, -1), out[1].reshape(1, 1, -1))  1.32 us

profile of v6, /device:TPU:1, one launch (start us, length us, event | category | flops | bytes accessed | tf_op | source)
XLA Modules:
  0.0 31.4 jit_solution(15622204011637911577)
XLA Ops:
  1.3 28.8 %group_posterior.1 = f32[2,16,128]{2,1,0:T(8,128)} custom-call(s32[1]{0:T(128)S(6)} %copy.9.count, bf16[6,6,128,384]{3,2,1,0:T(8,128)(2,1)} %bitcast.7, bf16[3,3,3,64,64]{4,3,2,1,0:T(8,128)(2,1)} %weight.1, f32[1,64]{1,0:T(1,128)} %bitcast.12, s32[1,2048]{1,0:T(1,128)} %bitcast.8, f32[1,2048]{1,0:T(1,128)} %bitcast.9, s32[1,64]{1,0:T(1,128)} %bitcast.13), custom_call_target="tpu_custom_call" | custom-call | tf_op jit(solution)/shard_map/group_posterior/pallas_call | solution.py:320
  30.0 1.3 %fusion = (f32[1,16,128]{2,1,0:T(8,128)}, f32[1,16,128]{2,1,0:T(8,128)}) fusion(f32[2,16,128]{2,1,0:T(8,128)} %group_posterior.1), kind=kLoop, calls=%fused_computation | loop fusion | bytes 32768 | tf_op jit(solution)/shard_map/slice | solution.py:359

commit v7 on v6

--- a/solution.py
+++ b/solution.py
@@ -170,7 +170,10 @@
         l_hi, l_lo = split2(low)
         part = dot(jnp.concatenate([l_hi, l_lo], axis=0), t_hi[...])
         rest = rest - (part[:n] + (part[n:] + dot(l_hi, t_lo[...])))
-    rows = dot(inverse_factor(gram), rest, 1, 0, HIGHEST)
+    i_hi, i_lo = split2(inverse_factor(gram))
+    b_hi, b_lo = split2(rest)
+    part = dot(jnp.concatenate([i_hi, i_lo], axis=0), b_hi)
+    rows = part[:n] + (part[n:] + dot(i_hi, b_lo))
     r_hi, r_lo = split2(rows)
     t_hi[at : at + n, :] = r_hi
     t_lo[at : at + n, :] = r_lo
@@ -237,10 +240,6 @@
                 remote(aux, sides.at[i + 1], ssend.at[i], srecv.at[i], (g, z)),
             )
         )
-    for codes, side in hops:
-        side.start()
-        codes.start()
-
     half = NQ // 2
     top, bottom = pl.ds(0, half), pl.ds(half, half)
     near = [
@@ -263,6 +262,10 @@
             pieces.append(remote(piece, piece, csend.at[2 * i + j], crecv.at[2 * i + j], (other, m)))
     for copy in near:
         copy.start()
+
+    for codes, side in hops:
+        side.start()
+        codes.start()
 
     def step(slots, at):
         for slot in slots:

time: 31.9 us -> 31.6 us (level)
  no operation moved by 1% of the time
where the time goes in v7:
time: 31.6 us; the launch traced here: 31.2 us
  Pallas kernels  28.6 us (91%)
  local copies, waits for them, and re-layouts  1.32 us (4%)
  between operations  1.29 us (4%)
    pallas_call x1, Pallas kernels, group_posterior(): pl.pallas_call(functools.partial(group_kernel, n_mem), out_shape=jax.Shap...  28.6 us
    slice x1, local copies, waits for them, and re-layouts, on_device(): return (out[0].reshape(1, 1, -1), out[1].reshape(1, 1, -1))  1.32 us

profile of v7, /device:TPU:1, one launch (start us, length us, event | category | flops | bytes accessed | tf_op | source)
XLA Modules:
  0.0 31.2 jit_solution(1915405902802730977)
XLA Ops:
  1.3 28.6 %group_posterior.1 = f32[2,16,128]{2,1,0:T(8,128)} custom-call(s32[1]{0:T(128)S(6)} %copy.9.count, bf16[6,6,128,384]{3,2,1,0:T(8,128)(2,1)} %bitcast.7, bf16[3,3,3,64,64]{4,3,2,1,0:T(8,128)(2,1)} %weight.1, f32[1,64]{1,0:T(1,128)} %bitcast.12, s32[1,2048]{1,0:T(1,128)} %bitcast.8, f32[1,2048]{1,0:T(1,128)} %bitcast.9, s32[1,64]{1,0:T(1,128)} %bitcast.13), custom_call_target="tpu_custom_call" | custom-call | tf_op jit(solution)/shard_map/group_posterior/pallas_call | solution.py:323
  29.9 1.3 %fusion = (f32[1,16,128]{2,1,0:T(8,128)}, f32[1,16,128]{2,1,0:T(8,128)}) fusion(f32[2,16,128]{2,1,0:T(8,128)} %group_posterior.1), kind=kLoop, calls=%fused_computation | loop fusion | bytes 32768 | tf_op jit(solution)/shard_map/slice | solution.py:362
